TPU v7x, 32 devices: a whole 2x2x4 slice. The times are simulated.
32 devices in a mesh: stream: 16 (over z, y, x), cross: 2 (over core).
Axes of the slice: x: 2, y: 2, z: 4, core: 2. Of those that a mesh axis runs over, the one named last changes fastest.
Arguments:
- vector: float32 [64, 4, 320], P('stream', 'cross'), may hold values from -2.5 to 2.5
- inverses: float32 [64, 4, 320, 320], P('stream', 'cross'), may hold values from -0.04 to 1
- lift_maps: float32 [4, 320, 80], replicated, may hold values from -1 to 1
- jacobians: float32 [64, 4, 4, 5, 5, 16], P('stream', 'cross'), may hold values from -0.2 to 1.43
- orient: int32 [64, 4], P('stream', 'cross'), may hold values from 0 to 7
Outputs:
- solution: float32 [64, 4, 320], P('stream', 'cross')
All inputs are finite; a program needn't handle non-finite values.
Results may differ from a plain program's by a relative error of at most 0.0003.
Values sent between devices are 32-bit elements; how exact they have to be, the bound alone decides.
A program may use at most 64 MiB of HBM per device.

v0:
```python
import functools

import jax
import jax.numpy as jnp
import numpy as np
from jax import lax
from jax.experimental import pallas as pl
from jax.experimental.pallas import tpu as pltpu
from jax.sharding import PartitionSpec as P

ORDER = 3
EXTENT = ORDER + 1
VARS = 5
FACE = EXTENT * EXTENT
TRACE = VARS * FACE
BLOCK = VARS * FACE * EXTENT
SLOTS = (0, EXTENT - 1) + tuple(range(1, EXTENT - 1))
WIDE = 256
ROWS = TRACE + 8
F32 = jnp.float32
BF16 = jnp.bfloat16


def split(value):
    high = value.astype(BF16)
    return high, (value - high.astype(F32)).astype(BF16)


def product(left, right, transposed=False):
    dims = (((1,), (1 if transposed else 0,)), ((), ()))
    dot = functools.partial(lax.dot_general, dimension_numbers=dims, preferred_element_type=F32)
    left_high, left_low = left
    right_high, right_low = right
    return dot(left_high, right_high) + (dot(left_high, right_low) + dot(left_low, right_high))


def lanes(shape):
    return lax.broadcasted_iota(jnp.int32, shape, 1)


def rows(shape):
    return lax.broadcasted_iota(jnp.int32, shape, 0)


def keep(mask, value):
    return jnp.where(mask, value, 0.0)


def join(left, right):
    lane = lanes((TRACE, WIDE))
    through = jnp.concatenate(
        [jnp.zeros((TRACE, WIDE), F32), keep(lane < 2 * TRACE, right[:TRACE])], axis=0
    )
    first = product(split(left[:, : 2 * TRACE]), split(through))
    lane_all = lanes((ROWS, WIDE))
    row_all = rows((ROWS, WIDE))
    first = first + keep((lane_all >= 2 * TRACE) | (row_all >= TRACE), right)
    back = left[:TRACE]
    moved = pltpu.roll(back, WIDE - 2 * TRACE, 1)
    through = jnp.concatenate(
        [
            keep(lane < TRACE, moved),
            jnp.zeros((TRACE, WIDE), F32),
            keep(lane >= 2 * TRACE, back),
        ],
        axis=0,
    )
    second = product(split(first[:, : 3 * TRACE]), split(through))
    middle = (lane_all >= TRACE) & (lane_all < 2 * TRACE)
    return second + keep(middle, first) + keep(lane_all < TRACE, left)


def apply(column, matrix):
    return jnp.sum(column * matrix, axis=0, keepdims=True)


def stack(parts):
    total = jnp.zeros((8, parts[0].shape[1]), F32)
    row = rows(total.shape)
    for index, part in enumerate(parts):
        total = jnp.where(row == index, jnp.broadcast_to(part, total.shape), total)
    return total


def to_low(value):
    return keep(lanes(value.shape) < TRACE, pltpu.roll(value, WIDE - 2 * TRACE, 1))


def rise(z_left, z_right, left, right):
    lane = lanes((8, WIDE))
    column = z_left.T
    first = z_right + keep(
        lane < 2 * TRACE,
        stack([apply(column[TRACE : 2 * TRACE, c : c + 1], m) for c, m in enumerate(right)]),
    )
    column = first.T
    second = stack([apply(column[:TRACE, c : c + 1], m) for c, m in enumerate(left)])
    return to_low(second) + keep(lane < TRACE, z_left) + keep(lane >= TRACE, first)


def descend(z_in, z_left, z_right, left, right):
    lane = lanes((8, WIDE))
    high = (lane >= TRACE) & (lane < 2 * TRACE)
    column = z_in.T
    inner = keep(
        high,
        z_left + stack([apply(column[TRACE : 2 * TRACE, c : c + 1], m) for c, m in enumerate(left)]),
    )
    passed = stack([apply(column[:TRACE, c : c + 1], m) for c, m in enumerate(right)])
    column = inner.T
    turned = stack([apply(column[TRACE : 2 * TRACE, c : c + 1], m) for c, m in enumerate(right)])
    low = keep(lane < TRACE, z_right + turned) + to_low(passed)
    return low + keep(high, z_in), keep(lane < TRACE, z_in) + inner


def kernel(
    layers, cells, count, width, rounds,
    inv, vector, lift_maps, jacobians, orient, pick, out,
    blocks, block_sem, lhs, jac_rows, natural, lhs_high, lhs_low, lifted, ends, sides, y, x,
    nodes, z_nodes, mine, theirs, send_sem, recv_sem, tail_sems,
    z_mine, z_theirs, z_send, z_recv,
    turns, traces, backs, got_high, got_back, from_left, from_right, cross_sems,
):
    elements = layers * cells
    place = lax.axis_index("stream")
    column_at = lax.axis_index("cross")
    local = layers.bit_length() - 1

    copies = []
    for e in range(elements):
        for slot, i in enumerate(SLOTS):
            copy = pltpu.make_async_copy(inv.at[e, :, i], blocks.at[e, slot], block_sem.at[e, slot])
            copy.start()

    bits = [lax.rem(place // (1 << k), 2) for k in range(rounds)]
    partners = [place + (1 - 2 * bits[k]) * (1 << k) for k in range(rounds)]
    barrier = pltpu.get_barrier_semaphore()
    for k in range(rounds):
        pl.semaphore_signal(barrier, inc=1, device_id=(partners[k], column_at), device_id_type=pl.DeviceIdType.MESH)

    @pl.when(column_at > 0)
    def _():
        pl.semaphore_signal(barrier, inc=1, device_id=(place, column_at - 1), device_id_type=pl.DeviceIdType.MESH)

    @pl.when(column_at < width - 1)
    def _():
        pl.semaphore_signal(barrier, inc=1, device_id=(place, column_at + 1), device_id_type=pl.DeviceIdType.MESH)

    for m in range(4):
        lhs[m * TRACE : (m + 1) * TRACE, :] = lift_maps[m]
    lhs[4 * TRACE :, :] = jnp.zeros((lhs.shape[0] - 4 * TRACE, BLOCK), F32)
    for e in range(elements):
        lhs[4 * TRACE + e : 4 * TRACE + e + 1, :] = vector[e // cells, e % cells : e % cells + 1, :]
        for v in range(VARS):
            for w in range(VARS):
                jac_rows[e, w, :4, v * FACE : (v + 1) * FACE] = jacobians[e, v, w]
    high, low = split(lhs[...])
    lhs_high[...] = high
    lhs_low[...] = low
    z_nodes[...] = jnp.zeros_like(z_nodes)
    z_mine[...] = jnp.zeros_like(z_mine)
    backs[...] = jnp.zeros_like(backs)

    lane = lanes((TRACE, WIDE))

    row_face = rows((TRACE, TRACE))
    lane_face = lanes((TRACE, TRACE))
    same = lax.rem(row_face, FACE) == lax.rem(lane_face, FACE)

    def source_of(code, node_index):
        first = lax.div(node_index, EXTENT)
        second = node_index - first * EXTENT
        first, second = (
            first + lax.rem(code, 2) * (second - first),
            second + lax.rem(code, 2) * (first - second),
        )
        first = first + lax.rem(code // 2, 2) * (EXTENT - 1 - 2 * first)
        second = second + lax.rem(code // 4, 2) * (EXTENT - 1 - 2 * second)
        return first * EXTENT + second

    def face(e, m, chosen):
        tall = jnp.concatenate(
            [jnp.broadcast_to(jac_rows[e, w, m : m + 1, :TRACE], (FACE, TRACE)) for w in range(VARS)],
            axis=0,
        )
        return keep(chosen, tall)

    def prepare_layer(layer, carry):
        for c in range(cells):
            prepare(layer * cells + c)
        return carry

    def prepare(e):
        for slot, i in enumerate(SLOTS):
            pltpu.make_async_copy(inv.at[e, :, i], blocks.at[e, slot], block_sem.at[e, slot]).wait()
        block = split(blocks[e].reshape(BLOCK, BLOCK))
        through = product((lhs_high[...], lhs_low[...]), block, transposed=True)
        row_values = through[4 * TRACE : 4 * TRACE + elements]
        own = jnp.sum(keep(rows(row_values.shape) == e, row_values), axis=0, keepdims=True)
        y[pl.ds(e, 1), :] = own
        lifted[e] = through[2 * TRACE : 4 * TRACE]
        upward = -product(split(face(e, 0, same)), split(through[:TRACE]))
        downward = -product(split(face(e, 1, same)), split(through[TRACE : 2 * TRACE]))
        ends[e, :TRACE] = downward
        ends[e, TRACE:] = upward
        matrix = keep(lane < 2 * TRACE, upward[:, :WIDE]) + pltpu.roll(
            keep(lane < TRACE, downward[:, :WIDE]), 2 * TRACE, 1
        )
        nodes[e, :TRACE] = matrix
        bottom = keep(lanes((8, WIDE)) < 2 * TRACE, jnp.broadcast_to(own[:, :WIDE], (8, WIDE)))
        nodes[e, TRACE:] = keep(rows((8, WIDE)) == 0, bottom)

    lax.fori_loop(0, layers, prepare_layer, 0)

    sides_met = jnp.minimum(column_at, 1) + jnp.minimum(width - 1 - column_at, 1)
    pl.semaphore_wait(barrier, rounds + sides_met)

    starts = []
    base = 0
    for level in range(local + 1):
        starts.append(base)
        base += layers >> level

    def node(level, index, c):
        return (starts[level] + index) * cells + c

    def remote(source, target, send, recv, device):
        return pltpu.make_async_remote_copy(
            src_ref=source, dst_ref=target, send_sem=send, recv_sem=recv,
            device_id=device, device_id_type=pl.DeviceIdType.MESH,
        )

    sent = []
    pending = {}

    def dispatch(k, c):
        device = (partners[k], column_at)
        send, recv = send_sem.at[k, c], recv_sem.at[k, c]
        if k < rounds - 1:
            pending[k, c] = [remote(mine.at[k, c], theirs.at[k, c], send, recv, device)]
        else:
            first, second = pl.ds(0, 128), pl.ds(128, 128)
            bottom = pl.ds(TRACE, 8)
            pending[k, c] = [
                remote(mine.at[k, c, :, first], theirs.at[k, c, :, first], send, recv, device),
                remote(
                    mine.at[k, c, bottom, second], theirs.at[k, c, bottom, second],
                    tail_sems.at[0, c], tail_sems.at[1, c], device,
                ),
            ]
        for copy in pending[k, c]:
            copy.start()
            sent.append(copy)

    for c in range(cells):
        for level in range(local):
            for index in range(layers >> (level + 1)):
                nodes[node(level + 1, index, c)] = join(
                    nodes[node(level, 2 * index, c)], nodes[node(level, 2 * index + 1, c)]
                )
        mine[0, c] = nodes[node(local, 0, c)]
        dispatch(0, c)

    def prepare_sides(layer, carry):
        for c in range(cells):
            e = layer * cells + c
            chosen = lax.rem(row_face, FACE) == source_of(orient[c, layer], lax.rem(lane_face, FACE))
            sides[e, :TRACE] = product(split(face(e, 2, chosen)), split(lifted[e, :TRACE]))
            sides[e, TRACE:] = product(split(face(e, 3, same)), split(lifted[e, TRACE:]))
        return carry

    def prepare_turns(layer, carry):
        within = row_face - block_row * FACE
        for c in range(cells):
            turn = (block_row == block_lane) & (source_of(orient[c, layer], within) == face_lane)
            turns[layer * cells + c] = turn.astype(F32)
        return carry

    block_row, block_lane = lax.div(row_face, FACE), lax.div(lane_face, FACE)
    face_lane = lane_face - block_lane * FACE

    for k in range(rounds):
        if k == 0:
            lax.fori_loop(0, layers, prepare_sides, 0)
        if k == 1 % rounds:
            lax.fori_loop(0, layers, prepare_turns, 0)
        for c in range(cells):
            for copy in pending[k, c]:
                copy.wait_recv()
            if k < rounds - 1:
                flag = bits[k] == 1
                ours, other = mine[k, c], theirs[k, c]
                mine[k + 1, c] = join(jnp.where(flag, other, ours), jnp.where(flag, ours, other))
                dispatch(k + 1, c)

    def ordered(k, c):
        flag = bits[k] == 1
        ours, other = mine[k, c, :TRACE], theirs[k, c, :TRACE]
        return jnp.where(flag, other, ours), jnp.where(flag, ours, other)

    def fall(z_pairs):
        lane_z = lanes((8, WIDE))
        z_in = None
        for k in reversed(range(rounds)):
            flag = bits[k] == 1
            ours, other = z_pairs[k]
            z_left, z_right = jnp.where(flag, other, ours), jnp.where(flag, ours, other)
            if z_in is None:
                column = z_left.T
                turned = stack([
                    apply(column[TRACE : 2 * TRACE, c : c + 1], theirs[k, c, :TRACE, :128])
                    for c in range(cells)
                ])
                turned = jnp.concatenate([turned, jnp.zeros((8, WIDE - 128), F32)], axis=1)
                z_low = keep(lane_z < TRACE, z_right + turned)
                z_high = keep((lane_z >= TRACE) & (lane_z < 2 * TRACE), z_left)
            else:
                pairs = [ordered(k, c) for c in range(cells)]
                z_low, z_high = descend(
                    z_in, z_left, z_right, [p[0] for p in pairs], [p[1] for p in pairs]
                )
            z_in = jnp.where(flag, z_high, z_low)
        entering = [z_in]
        for level in reversed(range(local)):
            following = []
            for index in range(layers >> (level + 1)):
                left = [nodes[node(level, 2 * index, c), :TRACE] for c in range(cells)]
                right = [nodes[node(level, 2 * index + 1, c), :TRACE] for c in range(cells)]
                following += list(
                    descend(
                        entering[index],
                        z_nodes[starts[level] + 2 * index],
                        z_nodes[starts[level] + 2 * index + 1],
                        left,
                        right,
                    )
                )
            entering = following
        for layer in range(layers):
            column = entering[layer].T
            for c in range(cells):
                e = layer * cells + c
                x[e : e + 1, :] = y[e : e + 1, :] + apply(column[: 2 * TRACE, c : c + 1], ends[e])

    for level in range(local):
        for index in range(layers >> level):
            for c in range(cells):
                z_nodes[starts[level] + index, c : c + 1, :] = nodes[node(level, index, c), TRACE : TRACE + 1]
    fall([
        (
            stack([mine[k, c, TRACE : TRACE + 1] for c in range(cells)]),
            stack([theirs[k, c, TRACE : TRACE + 1] for c in range(cells)]),
        )
        for k in range(rounds)
    ])

    x_high, x_low = split(x[...])
    cross = jnp.dot(x_high, pick[...], preferred_element_type=F32) + jnp.dot(
        x_low, pick[...], preferred_element_type=F32
    )
    traces[...] = cross[:, 128:]
    column = cross[:, :128].T
    for e in range(elements):
        backs[e : e + 1, :TRACE] = apply(column[:TRACE, e : e + 1], turns[e])
    up = remote(traces, got_high, cross_sems.at[0], cross_sems.at[1], (place, lax.rem(column_at + 1, width)))
    down = remote(backs, got_back, cross_sems.at[2], cross_sems.at[3], (place, lax.rem(column_at + width - 1, width)))

    @pl.when(column_at < width - 1)
    def _():
        up.start()

    @pl.when(column_at > 0)
    def _():
        down.start()

    for layer in range(layers):
        for c in range(cells):
            e = layer * cells + c
            if c > 0:
                from_left[e : e + 1, :] = traces[e - 1 : e, :]
            if c < cells - 1:
                from_right[e : e + 1, :] = backs[e + 1 : e + 2, :]
    firsts = [layer * cells for layer in range(layers)]
    lasts = [layer * cells + cells - 1 for layer in range(layers)]

    @pl.when(column_at > 0)
    def _():
        up.wait_recv()
        for first, last in zip(firsts, lasts):
            from_left[first : first + 1, :] = got_high[last : last + 1, :]

    @pl.when(column_at == 0)
    def _():
        for first in firsts:
            from_left[first : first + 1, :] = jnp.zeros((1, 128), F32)

    @pl.when(column_at < width - 1)
    def _():
        down.wait_recv()
        for first, last in zip(firsts, lasts):
            from_right[last : last + 1, :] = got_back[first : first + 1, :]

    @pl.when(column_at == width - 1)
    def _():
        for last in lasts:
            from_right[last : last + 1, :] = jnp.zeros((1, 128), F32)

    left_columns = from_left[...].T
    right_columns = from_right[...].T
    lane_row = lanes((1, WIDE))
    for layer in range(layers):
        for c in range(cells):
            e = layer * cells + c
            value = y[e : e + 1, :] - (
                apply(left_columns[:TRACE, e : e + 1], sides[e, :TRACE])
                + apply(right_columns[:TRACE, e : e + 1], sides[e, TRACE:])
            )
            y[e : e + 1, :] = value
            z_nodes[starts[0] + layer, c : c + 1, :] = keep(lane_row < 2 * TRACE, value[:, :WIDE])

    for level in range(local):
        for index in range(layers >> (level + 1)):
            left = [nodes[node(level, 2 * index, c), :TRACE] for c in range(cells)]
            right = [nodes[node(level, 2 * index + 1, c), :TRACE] for c in range(cells)]
            z_nodes[starts[level + 1] + index] = rise(
                z_nodes[starts[level] + 2 * index], z_nodes[starts[level] + 2 * index + 1], left, right
            )
    z_mine[0] = z_nodes[starts[local]]
    for k in range(rounds):
        copy = remote(z_mine.at[k], z_theirs.at[k], z_send.at[k], z_recv.at[k], (partners[k], column_at))
        copy.start()
        sent.append(copy)
        if k < rounds - 1:
            pairs = [ordered(k, c) for c in range(cells)]
        copy.wait_recv()
        if k < rounds - 1:
            flag = bits[k] == 1
            ours, other = z_mine[k], z_theirs[k]
            z_mine[k + 1] = rise(
                jnp.where(flag, other, ours), jnp.where(flag, ours, other),
                [p[0] for p in pairs], [p[1] for p in pairs],
            )
    fall([(z_mine[k], z_theirs[k]) for k in range(rounds)])
    for slot, i in enumerate(SLOTS):
        for v in range(VARS):
            target = (v * EXTENT + i) * FACE
            source = slot * TRACE + v * FACE
            natural[:, target : target + FACE] = x[:, source : source + FACE]
    for layer in range(layers):
        out[layer] = natural[layer * cells : (layer + 1) * cells, :]

    for copy in sent:
        copy.wait_send()

    @pl.when(column_at < width - 1)
    def _():
        up.wait_send()

    @pl.when(column_at > 0)
    def _():
        down.wait_send()


def picker():
    table = np.zeros((BLOCK, WIDE), np.float32)
    for slot, i in enumerate(SLOTS):
        for v in range(VARS):
            for k in range(EXTENT):
                source = slot * TRACE + v * FACE + k
                target = v * FACE + i * EXTENT + k
                table[source, target] = 1.0
                table[source + (EXTENT - 1) * EXTENT, 128 + target] = 1.0
    return table


def on_device(width, count, vector, inverses, lift_maps, jacobians, orient):
    layers, cells = vector.shape[:2]
    elements = layers * cells
    rounds = count.bit_length() - 1
    inv = inverses.reshape(elements, VARS, EXTENT, FACE, BLOCK)
    flat = jacobians.transpose(0, 1, 3, 4, 2, 5).reshape(elements, VARS, VARS, 4, FACE)
    pick = jnp.asarray(picker(), BF16)
    total_nodes = 2 * layers - 1
    depth = 4 * TRACE + -(-elements // 16) * 16
    vmem = pl.BlockSpec(memory_space=pltpu.VMEM)
    result = pl.pallas_call(
        functools.partial(kernel, layers, cells, count, width, rounds),
        out_shape=jax.ShapeDtypeStruct((layers, cells, BLOCK), F32),
        in_specs=[
            pl.BlockSpec(memory_space=pltpu.HBM), vmem, vmem, vmem,
            pl.BlockSpec(memory_space=pltpu.SMEM), vmem,
        ],
        out_specs=vmem,
        scratch_shapes=[
            pltpu.VMEM((elements, EXTENT, VARS, FACE, BLOCK), F32),
            pltpu.SemaphoreType.DMA((elements, EXTENT)),
            pltpu.VMEM((depth, BLOCK), F32),
            pltpu.VMEM((elements, VARS, 8, 128), F32),
            pltpu.VMEM((elements, BLOCK), F32),
            pltpu.VMEM((depth, BLOCK), BF16),
            pltpu.VMEM((depth, BLOCK), BF16),
            pltpu.VMEM((elements, 2 * TRACE, BLOCK), F32),
            pltpu.VMEM((elements, 2 * TRACE, BLOCK), F32),
            pltpu.VMEM((elements, 2 * TRACE, BLOCK), F32),
            pltpu.VMEM((elements, BLOCK), F32),
            pltpu.VMEM((elements, BLOCK), F32),
            pltpu.VMEM((total_nodes * cells, ROWS, WIDE), F32),
            pltpu.VMEM((total_nodes, 8, WIDE), F32),
            pltpu.VMEM((rounds, cells, ROWS, WIDE), F32),
            pltpu.VMEM((rounds, cells, ROWS, WIDE), F32),
            pltpu.SemaphoreType.DMA((rounds, cells)),
            pltpu.SemaphoreType.DMA((rounds, cells)),
            pltpu.SemaphoreType.DMA((2, cells)),
            pltpu.VMEM((rounds, 8, WIDE), F32),
            pltpu.VMEM((rounds, 8, WIDE), F32),
            pltpu.SemaphoreType.DMA((rounds,)),
            pltpu.SemaphoreType.DMA((rounds,)),
            pltpu.VMEM((elements, TRACE, TRACE), F32),
            pltpu.VMEM((elements, 128), F32),
            pltpu.VMEM((elements, 128), F32),
            pltpu.VMEM((elements, 128), F32),
            pltpu.VMEM((elements, 128), F32),
            pltpu.VMEM((elements, 128), F32),
            pltpu.VMEM((elements, 128), F32),
            pltpu.SemaphoreType.DMA((4,)),
        ],
        compiler_params=pltpu.CompilerParams(
            collective_id=0, has_side_effects=True, vmem_limit_bytes=62 * 1024 * 1024
        ),
    )(inv, vector, lift_maps.transpose(0, 2, 1), flat, orient.T, pick)
    return result


def solution(mesh):
    in_specs = (
        P("stream", "cross", None),
        P("stream", "cross", None, None),
        P(),
        P("stream", "cross", None, None, None, None),
        P("stream", "cross"),
    )
    out_specs = P("stream", "cross", None)
    return jax.shard_map(
        functools.partial(on_device, mesh.shape["cross"], mesh.shape["stream"]),
        mesh=mesh, in_specs=in_specs, out_specs=out_specs, check_vma=False,
    )
```

profile of v0, /device:TPU:0, one launch (start us, length us, event | category | flops | bytes accessed | tf_op | source)
XLA Modules:
  0.0 52.7 jit_solution(4606105505033693001)
XLA Ops:
  0.0 51.4 %shard_map.64 = f32[4,2,320]{2,1,0:T(2,128)} custom-call(f32[8,5,4,16,320]{4,3,2,1,0:T(8,128)} %bitcast.6, f32[4,2,320]{2,1,0:T(2,128)} %vector.1, f32[4,80,320]{2,1,0:T(8,128)} %bitcast.7, f32[8,5,5,4,16]{4,3,2,1,0:T(4,128)} %bitcast.8, s32[2,4]{1,0:T(2,128)} %bitcast.9, bf16[320,256]{1,0:T(8,128)(2,1)} %constant.2.clone.pick), custom_call_target="tpu_custom_call" | custom-call | tf_op jit(solution)/shard_map/pallas_call | solution.py:486
  51.4 1.3 %copy.8 = f32[4,2,320]{2,1,0:T(2,128)} copy(f32[4,2,320]{2,1,0:T(2,128)} %shard_map.64) | data formatting | bytes 20480
where the time goes:
time: 53.4 us; the launch traced here: 52.7 us
  Pallas kernels  51.4 us (96%)
  local copies, waits for them, and re-layouts  1.31 us (2%)
    pallas_call x1, Pallas kernels, on_device(): pl.pallas_call(functools.partial(kernel, layers, cells, count, width, rou...  51.4 us
    unnamed x1, local copies, waits for them, and re-layouts  1.31 us

commit v1 on v0

v1 whole, which is shorter than its diff:
```python
import functools

import jax
import jax.numpy as jnp
import numpy as np
from jax import lax
from jax.experimental import pallas as pl
from jax.experimental.pallas import tpu as pltpu
from jax.sharding import PartitionSpec as P

ORDER = 3
EXTENT = ORDER + 1
VARS = 5
FACE = EXTENT * EXTENT
TRACE = VARS * FACE
BLOCK = VARS * FACE * EXTENT
HALF = BLOCK // 2
SLOTS = (0, EXTENT - 1) + tuple(range(1, EXTENT - 1))
WIDE = 256
ROWS = TRACE + 8
F32 = jnp.float32
BF16 = jnp.bfloat16


def split(value):
    high = value.astype(BF16)
    return high, (value - high.astype(F32)).astype(BF16)


def product(left, right, transposed=False):
    dims = (((1,), (1 if transposed else 0,)), ((), ()))
    dot = functools.partial(lax.dot_general, dimension_numbers=dims, preferred_element_type=F32)
    left_high, left_low = left
    right_high, right_low = right
    return dot(left_high, right_high) + (dot(left_high, right_low) + dot(left_low, right_high))


def spread(value):
    wide = BLOCK - BLOCK % WIDE
    high_part, low_part = split(value)
    none = jnp.zeros((value.shape[0], WIDE - 3 * (BLOCK - wide)), BF16)
    return (high_part[:, :wide], low_part[:, :wide]), (high_part[:, wide:], low_part[:, wide:]), none


def pack_left(value):
    (body_high, body_low), (tail_high, tail_low), none = spread(value)
    return jnp.concatenate([body_high, body_high, body_low, tail_high, tail_high, tail_low, none], axis=1)


def pack_right(value):
    (body_high, body_low), (tail_high, tail_low), none = spread(value)
    return jnp.concatenate([body_high, body_low, body_high, tail_high, tail_low, tail_high, none], axis=1)


def against(left, right):
    return lax.dot_general(left, right, (((1,), (1,)), ((), ())), preferred_element_type=F32)


def faced(face, value):
    high_part, low_part = split(value)
    return jnp.dot(
        face, jnp.concatenate([high_part, low_part, high_part], axis=0), preferred_element_type=F32
    )


def multiply(left, right):
    return product(split(left), split(right))


def lanes(shape):
    return lax.broadcasted_iota(jnp.int32, shape, 1)


def rows(shape):
    return lax.broadcasted_iota(jnp.int32, shape, 0)


def keep(mask, value):
    return jnp.where(mask, value, 0.0)


def low(value):
    return keep(lanes(value.shape) < TRACE, value)


def high(value):
    lane = lanes(value.shape)
    return keep((lane >= TRACE) & (lane < 2 * TRACE), value)


def below(value):
    return jnp.concatenate([jnp.zeros((TRACE, value.shape[1]), F32), value], axis=0)


def to_low(value):
    return low(pltpu.roll(value, WIDE - 2 * TRACE, 1))


def join(left, right):
    lane = lanes((TRACE, WIDE))
    through = below(keep(lane < 2 * TRACE, right[:TRACE]))
    first = multiply(left[:, : 2 * TRACE], through)
    lane_all = lanes((ROWS, WIDE))
    row_all = rows((ROWS, WIDE))
    first = first + keep((lane_all >= 2 * TRACE) | (row_all >= TRACE), right)
    back = left[:TRACE]
    through = jnp.concatenate(
        [to_low(back), jnp.zeros((TRACE, WIDE), F32), keep(lane >= 2 * TRACE, back)], axis=0
    )
    second = multiply(first[:, : 3 * TRACE], through)
    middle = (lane_all >= TRACE) & (lane_all < 2 * TRACE)
    return first, second + keep(middle, first) + keep(lane_all < TRACE, left)


def apply(column, matrix):
    return jnp.sum(column * matrix, axis=0, keepdims=True)


def stack(parts):
    total = jnp.zeros((8, parts[0].shape[1]), F32)
    row = rows(total.shape)
    for index, part in enumerate(parts):
        total = jnp.where(row == index, jnp.broadcast_to(part, total.shape), total)
    return total


def each(z, matrices):
    pieces = split(z[:, : 2 * TRACE])
    row = rows((8, WIDE))
    total = jnp.zeros((8, WIDE), F32)
    for index, matrix in enumerate(matrices):
        total = jnp.where(row == index, product(pieces, split(matrix)), total)
    return total


def kernel(
    layers, cells, width, rounds,
    inv, vector, lift_maps, jacobians, orient, pick_source, out,
    blocks, block_sem, lifts, lift_sem, pick, pick_sem, vecs, jac_rows, packed, near,
    ends, sides, inner, full, y, x, entry, climb, reach, zmat, firsts,
    mine, theirs, send_sem, recv_sem, tail_sems, z_mine, z_theirs, z_send, z_recv,
    turns, traces, backs, got_high, got_back, from_left, from_right, cross_sems, natural,
):
    elements = layers * cells
    place = lax.axis_index("stream")
    column_at = lax.axis_index("cross")
    last = layers - 1
    vec_rows = vecs.shape[0]

    def at(layer, c):
        return layer * cells + c

    order = [at(layer, c) for c in range(cells) for layer in range(layers)]

    lift_copies = [
        pltpu.make_async_copy(lift_maps.at[2 * h : 2 * h + 2], lifts.at[2 * h : 2 * h + 2], lift_sem.at[h])
        for h in range(2)
    ]

    def block_copies(e, slots):
        return [
            pltpu.make_async_copy(inv.at[e, :, SLOTS[s]], blocks.at[e, s], block_sem.at[e, s]) for s in slots
        ]

    early, late = (0, 1), tuple(range(2, EXTENT))
    lift_copies[0].start()
    for e in order:
        for copy in block_copies(e, early):
            copy.start()
    pick_copy = pltpu.make_async_copy(pick_source, pick, pick_sem.at[0])

    bits = [lax.rem(place // (1 << k), 2) for k in range(rounds)]
    partners = [place + (1 - 2 * bits[k]) * (1 << k) for k in range(rounds)]
    barrier = pltpu.get_barrier_semaphore()
    for k in range(rounds):
        pl.semaphore_signal(barrier, inc=1, device_id=(partners[k], column_at), device_id_type=pl.DeviceIdType.MESH)

    @pl.when(column_at > 0)
    def _():
        pl.semaphore_signal(barrier, inc=1, device_id=(place, column_at - 1), device_id_type=pl.DeviceIdType.MESH)

    @pl.when(column_at < width - 1)
    def _():
        pl.semaphore_signal(barrier, inc=1, device_id=(place, column_at + 1), device_id_type=pl.DeviceIdType.MESH)

    vecs[...] = jnp.zeros_like(vecs)
    jac_rows[...] = jnp.zeros_like(jac_rows)
    for e in range(elements):
        vecs[e : e + 1, :] = vector[e // cells, e % cells : e % cells + 1, :]
        for v in range(VARS):
            for w in range(VARS):
                jac_rows[e, w, :4, v * FACE : (v + 1) * FACE] = jacobians[e, v, w]
        for w in range(VARS):
            value = jac_rows[e, w]
            jac_rows[e, w] = value + pltpu.roll(value, TRACE, 1) + pltpu.roll(value, 2 * TRACE, 1)
    ends[...] = jnp.zeros_like(ends)
    sides[...] = jnp.zeros_like(sides)
    y[...] = jnp.zeros_like(y)
    backs[...] = jnp.zeros_like(backs)

    row_face = rows((TRACE, TRACE))
    lane_face = lanes((TRACE, TRACE))
    row_wide = lax.rem(rows((TRACE, WIDE)), FACE)
    lane_wide = lax.rem(lanes((TRACE, WIDE)), FACE)
    same = row_wide == lane_wide
    leading = lanes((TRACE, WIDE)) < 2 * TRACE
    eye = rows((TRACE, WIDE)) == lanes((TRACE, WIDE))
    eye_low = eye.astype(F32)
    eye_high = (rows((TRACE, WIDE)) + TRACE == lanes((TRACE, WIDE))).astype(F32)
    first_row = rows((8, WIDE)) == 0

    def source_of(code, node_index):
        first = lax.div(node_index, EXTENT)
        second = node_index - first * EXTENT
        first, second = (
            first + lax.rem(code, 2) * (second - first),
            second + lax.rem(code, 2) * (first - second),
        )
        first = first + lax.rem(code // 2, 2) * (EXTENT - 1 - 2 * first)
        second = second + lax.rem(code // 4, 2) * (EXTENT - 1 - 2 * second)
        return first * EXTENT + second

    def face(e, m, chosen):
        tall = jnp.concatenate(
            [jnp.broadcast_to(jac_rows[e, w, m : m + 1, :], (FACE, WIDE)) for w in range(VARS)],
            axis=0,
        )
        value = keep(chosen, tall)
        value = jnp.where(leading, value, value - value.astype(BF16).astype(F32))
        return value[:, : 3 * TRACE].astype(BF16)

    def half(e, h):
        return pack_right(blocks[e, 2 * h : 2 * h + 2].reshape(HALF, BLOCK))

    def ending(e, h, through):
        ends[e, h, TRACE:, :HALF] = -faced(face(e, 0, same), through[:TRACE])
        ends[e, h, :TRACE, :HALF] = -faced(face(e, 1, same), through[TRACE : 2 * TRACE])

    vec_at, rest_at = 2 * TRACE, 2 * TRACE + vec_rows
    packed[vec_at:rest_at] = pack_left(vecs[...])
    lift_copies[0].wait()
    packed[:vec_at] = pack_left(lifts[0:2].reshape(2 * TRACE, BLOCK))

    def critical(e):
        block = half(e, 0)
        near[e] = block
        through = against(packed[:rest_at], block)
        y[0, e : e + 1, :HALF] = through[vec_at + e : vec_at + e + 1]
        ending(e, 0, through)

    def rest(e):
        through = against(packed[...], half(e, 1))
        y[1, e : e + 1, :HALF] = through[vec_at + e : vec_at + e + 1]
        ending(e, 1, through)
        chosen = row_wide == source_of(orient[e % cells, e // cells], lane_wide)
        faces = face(e, 2, chosen), face(e, 3, same)
        for h, value in enumerate((against(packed[rest_at:], near[e]), through[rest_at:])):
            for m in range(2):
                sides[e, h, m * TRACE : (m + 1) * TRACE, :HALF] = faced(
                    faces[m], value[m * TRACE : (m + 1) * TRACE]
                )

    def finish(e):
        for h in range(2):
            full[e, h] = product(split(inner[e, :, : 2 * TRACE]), split(ends[e, h]))

    def chain(c):
        up = [ends[at(layer, c), 0, TRACE:] for layer in range(layers)]
        down = [ends[at(layer, c), 0, :TRACE] for layer in range(layers)]

        def bottom(layer):
            e = at(layer, c)
            return keep(first_row, jnp.broadcast_to(y[0, e : e + 1, :], (8, WIDE)))

        forward = [jnp.concatenate([up[0], bottom(0)], axis=0)]
        for layer in range(1, layers):
            step = multiply(forward[-1][:, : 2 * TRACE], below(up[layer]))
            forward.append(step + below(bottom(layer)))
            yield
        none = jnp.zeros((ROWS, WIDE), F32)
        backward = jnp.concatenate([eye_low, none], axis=0)
        for layer in reversed(range(layers)):
            before = forward[layer - 1] if layer else jnp.concatenate([eye_high, none[TRACE:]], axis=0)
            inner[at(layer, c)] = backward + below(high(before))
            if layer == last:
                backward = low(jnp.concatenate([down[layer], forward[layer]], axis=0))
            else:
                backward = low(multiply(backward[:, :TRACE], down[layer]) + below(forward[layer]))
                yield
        whole = backward[TRACE:] + high(forward[last])
        extra = pltpu.roll(backward[:TRACE], 2 * TRACE, 1)
        mine[0, c, TRACE:] = whole[TRACE:]
        mine[0, c, :TRACE] = whole[:TRACE] + extra

    def responses(c):
        behind = eye_low
        reach_low, after = [], []
        for layer in range(layers):
            reach_low.append(behind)
            e = at(layer, c)
            pair = jnp.concatenate([ends[e, 0, TRACE:], ends[e, 0, :TRACE]], axis=0)
            if layer == 0:
                both = low(pair)
            else:
                both = low(multiply(pair[:, :TRACE], behind))
            after.append(both[:TRACE])
            behind = both[TRACE:]
        ahead = eye_high
        for layer in reversed(range(layers)):
            e = at(layer, c)
            zmat[e, :TRACE] = reach_low[layer]
            zmat[e, TRACE:] = ahead
            if layer:
                if layer == last:
                    ahead = high(ends[e, 0, TRACE:]) + after[layer]
                else:
                    ahead = multiply(ends[e, 0, TRACE:, : 2 * TRACE], below(ahead)) + after[layer]

    def ordered(k, c):
        flag = bits[k] == 1
        ours, other = mine[k, c], theirs[k, c]
        return jnp.where(flag, other, ours), jnp.where(flag, ours, other)

    def reaching(k, c, first):
        flag = bits[k] == 1
        if k == 0:
            near, far = eye_low, low(first)
            ahead = eye_high
        else:
            near, ahead = entry[c, :TRACE], entry[c, TRACE : 2 * TRACE]
            far = multiply(first[:, :TRACE], near)
        reach[k, c, :TRACE] = jnp.where(flag, 0.0, near)
        reach[k, c, TRACE:] = jnp.where(flag, ahead, far)

    def level(k, c):
        left, right = ordered(k, c)
        reaching(k, c, right[:TRACE])
        flag = bits[k] == 1
        first = firsts[k, c]
        step = jnp.concatenate(
            [
                jnp.where(flag, eye_low, to_low(right[:TRACE])),
                jnp.where(flag, high(left[:TRACE]), low(first[:TRACE]) + eye_high),
                jnp.where(flag, high(left[TRACE:]), low(first[TRACE:])),
            ],
            axis=0,
        )
        if k == 0:
            entry[c] = step
        else:
            old = entry[c]
            moved = multiply(step[:, : 2 * TRACE], old[: 2 * TRACE])
            entry[c, : 2 * TRACE] = moved[: 2 * TRACE]
            entry[c, 2 * TRACE :] = moved[2 * TRACE :] + old[2 * TRACE :]
        back = to_low(left[:TRACE])
        climb[k, c, :TRACE] = back
        climb[k, c, TRACE:] = multiply(right[:TRACE, :TRACE], back) + high(right[:TRACE])

    block_row, block_lane = lax.div(row_face, FACE), lax.div(lane_face, FACE)
    face_lane = lane_face - block_lane * FACE

    def turn(e):
        within = row_face - block_row * FACE
        chosen = (block_row == block_lane) & (source_of(orient[e % cells, e // cells], within) == face_lane)
        turns[e] = chosen.astype(F32)

    def remote(source, target, send, recv, device):
        return pltpu.make_async_remote_copy(
            src_ref=source, dst_ref=target, send_sem=send, recv_sem=recv,
            device_id=device, device_id_type=pl.DeviceIdType.MESH,
        )

    sent = []
    pending = {}

    def dispatch(k, c):
        device = (partners[k], column_at)
        send, recv = send_sem.at[k, c], recv_sem.at[k, c]
        if k < rounds - 1:
            pending[k, c] = [remote(mine.at[k, c], theirs.at[k, c], send, recv, device)]
        else:
            one, two = pl.ds(0, 128), pl.ds(128, 128)
            foot = pl.ds(TRACE, 8)
            pending[k, c] = [
                remote(mine.at[k, c, :, one], theirs.at[k, c, :, one], send, recv, device),
                remote(
                    mine.at[k, c, foot, two], theirs.at[k, c, foot, two],
                    tail_sems.at[0, c], tail_sems.at[1, c], device,
                ),
            ]
        for copy in pending[k, c]:
            copy.start()
            sent.append(copy)

    sides_met = jnp.minimum(column_at, 1) + jnp.minimum(width - 1 - column_at, 1)
    def column_of(c):
        return [at(layer, c) for layer in range(layers)]

    def ready(members, slots):
        for e in members:
            for copy in block_copies(e, slots):
                copy.wait()

    ready(column_of(0), early)
    lift_copies[1].start()
    for e in order:
        for copy in block_copies(e, late):
            copy.start()
    pick_copy.start()
    for e in column_of(0):
        critical(e)
    for c in range(cells):
        steps = chain(c)
        if c + 1 < cells:
            ready(column_of(c + 1), early)
            for e in column_of(c + 1):
                next(steps, None)
                critical(e)
        for _ in steps:
            pass
        if c == 0:
            pl.semaphore_wait(barrier, rounds + sides_met)
        dispatch(0, c)

    lift_copies[1].wait()
    packed[rest_at:] = pack_left(lifts[2:4].reshape(2 * TRACE, BLOCK))
    ready(order, late)
    if rounds == 1:
        for c in range(cells):
            entry[c] = jnp.concatenate([eye_low, eye_high, jnp.zeros((8, WIDE), F32)], axis=0)

    tasks = []
    for index, e in enumerate(order):
        tasks.append(functools.partial(rest, e))
        if index:
            tasks.append(functools.partial(finish, order[index - 1]))
    tasks.append(functools.partial(finish, order[-1]))
    for e in range(elements):
        tasks.append(functools.partial(turn, e))
    for c in range(cells):
        tasks.append(functools.partial(responses, c))

    slots = rounds * cells
    quota = -(-len(tasks) // slots)

    def work(count):
        for _ in range(min(count, len(tasks))):
            tasks.pop(0)()

    for k in range(rounds):
        for c in range(cells):
            work(quota)
            for copy in pending[k, c]:
                copy.wait_recv()
            if k < rounds - 1:
                left, right = ordered(k, c)
                first, node = join(left, right)
                mine[k + 1, c] = node
                dispatch(k + 1, c)
                firsts[k, c] = first
                level(k, c)
    work(len(tasks))

    top = rounds - 1
    top_flag = bits[top] == 1

    def meet(z_ours, z_other, flag):
        z_left, z_right = jnp.where(flag, z_other, z_ours), jnp.where(flag, z_ours, z_other)
        return low(z_right) + high(z_left), low(z_left) + high(z_right)

    z_ours = stack([mine[top, c, TRACE : TRACE + 1] for c in range(cells)])
    z_other = stack([theirs[top, c, TRACE : TRACE + 1] for c in range(cells)])
    met, _ = meet(z_ours, z_other, top_flag)
    turned = each(met, [below(low(theirs[top, c, :TRACE])) for c in range(cells)])
    arrived = jnp.where(top_flag, high(met), low(met + turned))
    z_in = each(arrived, [entry[c, : 2 * TRACE] for c in range(cells)]) + stack(
        [entry[c, 2 * TRACE : 2 * TRACE + 1] for c in range(cells)]
    )
    column = z_in.T
    for layer in range(layers):
        for c in range(cells):
            e = at(layer, c)
            for h in range(2):
                x[h, e : e + 1, :] = (
                    y[h, e : e + 1, :]
                    + full[e, h, 2 * TRACE : 2 * TRACE + 1]
                    + apply(column[: 2 * TRACE, c : c + 1], full[e, h, : 2 * TRACE])
                )

    pick_copy.wait()
    cross = jnp.zeros((elements, WIDE), F32)
    for h in range(2):
        x_high, x_low = split(x[h])
        cross = cross + (
            jnp.dot(x_high, pick[h], preferred_element_type=F32)
            + jnp.dot(x_low, pick[h], preferred_element_type=F32)
        )
    traces[...] = cross[:, 128:]
    column = cross[:, :128].T
    for e in range(elements):
        backs[e : e + 1, :TRACE] = apply(column[:TRACE, e : e + 1], turns[e])
    up = remote(traces, got_high, cross_sems.at[0], cross_sems.at[1], (place, lax.rem(column_at + 1, width)))
    down = remote(backs, got_back, cross_sems.at[2], cross_sems.at[3], (place, lax.rem(column_at + width - 1, width)))

    @pl.when(column_at < width - 1)
    def _():
        up.start()

    @pl.when(column_at > 0)
    def _():
        down.start()

    for c in range(cells):
        reaching(top, c, jnp.concatenate([theirs[top, c, :TRACE, :128], jnp.zeros((TRACE, WIDE - 128), F32)], axis=1))
    for layer in range(layers):
        for c in range(cells):
            e = at(layer, c)
            if c > 0:
                from_left[e : e + 1, :] = traces[e - 1 : e, :]
            if c < cells - 1:
                from_right[e : e + 1, :] = backs[e + 1 : e + 2, :]
    firsts_at = [layer * cells for layer in range(layers)]
    lasts_at = [layer * cells + cells - 1 for layer in range(layers)]

    @pl.when(column_at > 0)
    def _():
        up.wait_recv()
        for one, two in zip(firsts_at, lasts_at):
            from_left[one : one + 1, :] = got_high[two : two + 1, :]

    @pl.when(column_at == 0)
    def _():
        for one in firsts_at:
            from_left[one : one + 1, :] = jnp.zeros((1, 128), F32)

    @pl.when(column_at < width - 1)
    def _():
        down.wait_recv()
        for one, two in zip(firsts_at, lasts_at):
            from_right[two : two + 1, :] = got_back[one : one + 1, :]

    @pl.when(column_at == width - 1)
    def _():
        for two in lasts_at:
            from_right[two : two + 1, :] = jnp.zeros((1, 128), F32)

    left_columns = from_left[...].T
    right_columns = from_right[...].T

    def loaded(e, h):
        return y[h, e : e + 1, :] - (
            apply(left_columns[:TRACE, e : e + 1], sides[e, h, :TRACE])
            + apply(right_columns[:TRACE, e : e + 1], sides[e, h, TRACE:])
        )

    for e in range(elements):
        y[0, e : e + 1, :] = loaded(e, 0)
    columns = y[0].T
    z_mine[0] = stack([
        functools.reduce(
            jnp.add,
            [apply(columns[: 2 * TRACE, at(layer, c) : at(layer, c) + 1], zmat[at(layer, c)]) for layer in range(layers)],
        )
        for c in range(cells)
    ])

    state = {}

    def gathered(layer):
        return stack([y[0, at(layer, c) : at(layer, c) + 1, :] for c in range(cells)])

    def local_sweeps():
        forward = [gathered(0)]
        for layer in range(1, layers):
            step = each(forward[-1], [below(ends[at(layer, c), 0, TRACE:]) for c in range(cells)])
            forward.append(step + gathered(layer))
        backward = jnp.zeros((8, WIDE), F32)
        for layer in reversed(range(layers)):
            before = high(forward[layer - 1]) if layer else jnp.zeros((8, WIDE), F32)
            state[layer] = backward + before
            if layer == last:
                backward = low(forward[layer])
            elif layer:
                inverse = [
                    jnp.concatenate([ends[at(layer, c), 0, :TRACE], jnp.zeros((TRACE, WIDE), F32)], axis=0)
                    for c in range(cells)
                ]
                backward = low(each(backward, inverse) + forward[layer])

    def local_rest():
        for e in range(elements):
            y[1, e : e + 1, :] = loaded(e, 1)

    def local_apply():
        for layer in range(layers):
            column = state[layer].T
            for c in range(cells):
                e = at(layer, c)
                for h in range(2):
                    x[h, e : e + 1, :] = y[h, e : e + 1, :] + apply(column[: 2 * TRACE, c : c + 1], ends[e, h])

    tasks = [local_sweeps, local_rest, local_apply]
    z_in = jnp.zeros((8, WIDE), F32)
    for k in range(rounds):
        flag = bits[k] == 1
        copy = remote(z_mine.at[k], z_theirs.at[k], z_send.at[k], z_recv.at[k], (partners[k], column_at))
        copy.start()
        sent.append(copy)
        if k < rounds - 1:
            work(1)
        else:
            work(len(tasks))
        copy.wait_recv()
        met, kept = meet(z_mine[k], z_theirs[k], flag)
        if k < rounds - 1:
            z_mine[k + 1] = each(met, [climb[k, c] for c in range(cells)]) + kept
        z_in = z_in + each(met, [reach[k, c] for c in range(cells)])

    column = z_in.T
    for layer in range(layers):
        for c in range(cells):
            e = at(layer, c)
            for h in range(2):
                x[h, e : e + 1, :] = x[h, e : e + 1, :] + apply(
                    column[: 2 * TRACE, c : c + 1], full[e, h, : 2 * TRACE]
                )
    for slot, i in enumerate(SLOTS):
        for v in range(VARS):
            target = (v * EXTENT + i) * FACE
            source = (slot % 2) * TRACE + v * FACE
            natural[:, target : target + FACE] = x[slot // 2, :, source : source + FACE]
    for layer in range(layers):
        out[layer] = natural[layer * cells : (layer + 1) * cells, :]

    for copy in sent:
        copy.wait_send()

    @pl.when(column_at < width - 1)
    def _():
        up.wait_send()

    @pl.when(column_at > 0)
    def _():
        down.wait_send()


def picker():
    table = np.zeros((2, WIDE, WIDE), np.float32)
    for slot, i in enumerate(SLOTS):
        for v in range(VARS):
            for k in range(EXTENT):
                source = (slot % 2) * TRACE + v * FACE + k
                target = v * FACE + i * EXTENT + k
                table[slot // 2, source, target] = 1.0
                table[slot // 2, source + (EXTENT - 1) * EXTENT, 128 + target] = 1.0
    return table


def on_device(width, count, vector, inverses, lift_maps, jacobians, orient):
    layers, cells = vector.shape[:2]
    elements = layers * cells
    rounds = count.bit_length() - 1
    inv = inverses.reshape(elements, VARS, EXTENT, FACE, BLOCK)
    flat = jacobians.transpose(0, 1, 3, 4, 2, 5).reshape(elements, VARS, VARS, 4, FACE)
    pick = jnp.asarray(picker(), BF16)
    vec_rows = -(-elements // 16) * 16
    depth = 4 * TRACE + vec_rows
    vmem = pl.BlockSpec(memory_space=pltpu.VMEM)
    hbm = pl.BlockSpec(memory_space=pltpu.HBM)
    tall = 2 * TRACE + 8
    result = pl.pallas_call(
        functools.partial(kernel, layers, cells, width, rounds),
        out_shape=jax.ShapeDtypeStruct((layers, cells, BLOCK), F32),
        in_specs=[hbm, vmem, hbm, vmem, pl.BlockSpec(memory_space=pltpu.SMEM), hbm],
        out_specs=vmem,
        scratch_shapes=[
            pltpu.VMEM((elements, EXTENT, VARS, FACE, BLOCK), F32),
            pltpu.SemaphoreType.DMA((elements, EXTENT)),
            pltpu.VMEM((4, TRACE, BLOCK), F32),
            pltpu.SemaphoreType.DMA((2,)),
            pltpu.VMEM((2, WIDE, WIDE), BF16),
            pltpu.SemaphoreType.DMA((1,)),
            pltpu.VMEM((vec_rows, BLOCK), F32),
            pltpu.VMEM((elements, VARS, 8, WIDE), F32),
            pltpu.VMEM((depth, 4 * WIDE), BF16),
            pltpu.VMEM((elements, HALF, 4 * WIDE), BF16),
            pltpu.VMEM((elements, 2, 2 * TRACE, WIDE), F32),
            pltpu.VMEM((elements, 2, 2 * TRACE, WIDE), F32),
            pltpu.VMEM((elements, tall, WIDE), F32),
            pltpu.VMEM((elements, 2, tall, WIDE), F32),
            pltpu.VMEM((2, elements, WIDE), F32),
            pltpu.VMEM((2, elements, WIDE), F32),
            pltpu.VMEM((cells, tall, WIDE), F32),
            pltpu.VMEM((rounds, cells, 2 * TRACE, WIDE), F32),
            pltpu.VMEM((rounds, cells, 2 * TRACE, WIDE), F32),
            pltpu.VMEM((elements, 2 * TRACE, WIDE), F32),
            pltpu.VMEM((rounds, cells, ROWS, WIDE), F32),
            pltpu.VMEM((rounds, cells, ROWS, WIDE), F32),
            pltpu.VMEM((rounds, cells, ROWS, WIDE), F32),
            pltpu.SemaphoreType.DMA((rounds, cells)),
            pltpu.SemaphoreType.DMA((rounds, cells)),
            pltpu.SemaphoreType.DMA((2, cells)),
            pltpu.VMEM((rounds, 8, WIDE), F32),
            pltpu.VMEM((rounds, 8, WIDE), F32),
            pltpu.SemaphoreType.DMA((rounds,)),
            pltpu.SemaphoreType.DMA((rounds,)),
            pltpu.VMEM((elements, TRACE, TRACE), F32),
            pltpu.VMEM((elements, 128), F32),
            pltpu.VMEM((elements, 128), F32),
            pltpu.VMEM((elements, 128), F32),
            pltpu.VMEM((elements, 128), F32),
            pltpu.VMEM((elements, 128), F32),
            pltpu.VMEM((elements, 128), F32),
            pltpu.SemaphoreType.DMA((4,)),
            pltpu.VMEM((elements, BLOCK), F32),
        ],
        compiler_params=pltpu.CompilerParams(
            collective_id=0, has_side_effects=True, vmem_limit_bytes=62 * 1024 * 1024
        ),
    )(inv, vector, lift_maps.transpose(0, 2, 1), flat, orient.T, pick)
    return result


def solution(mesh):
    in_specs = (
        P("stream", "cross", None),
        P("stream", "cross", None, None),
        P(),
        P("stream", "cross", None, None, None, None),
        P("stream", "cross"),
    )
    out_specs = P("stream", "cross", None)
    return jax.shard_map(
        functools.partial(on_device, mesh.shape["cross"], mesh.shape["stream"]),
        mesh=mesh, in_specs=in_specs, out_specs=out_specs, check_vma=False,
    )
```

time: 53.4 us -> 46.7 us (0.87)
  Pallas kernels: 51.4 us -> 45 us
    pallas_call x1, Pallas kernels: 51.4 us -> 45 us  [on_device(): pl.pallas_call(functools.partial(kernel, layers, cells, width, rounds), o...]
where the time goes in v1:
time: 46.7 us; the launch traced here: 46.4 us
  Pallas kernels  45 us (96%)
  local copies, waits for them, and re-layouts  1.31 us (3%)
    pallas_call x1, Pallas kernels, on_device(): pl.pallas_call(functools.partial(kernel, layers, cells, width, rounds), o...  45 us
    unnamed x1, local copies, waits for them, and re-layouts  1.31 us

profile of v1, /device:TPU:0, one launch (start us, length us, event | category | flops | bytes accessed | tf_op | source)
XLA Modules:
  0.0 46.4 jit_solution(11784461354455740690)
XLA Ops:
  0.0 45.0 %shard_map.64 = f32[4,2,320]{2,1,0:T(2,128)} custom-call(f32[8,5,4,16,320]{4,3,2,1,0:T(8,128)} %bitcast.6, f32[4,2,320]{2,1,0:T(2,128)} %vector.1, f32[4,80,320]{2,1,0:T(8,128)} %bitcast.7, f32[8,5,5,4,16]{4,3,2,1,0:T(4,128)} %bitcast.8, s32[2,4]{1,0:T(2,128)} %bitcast.9, bf16[2,256,256]{2,1,0:T(8,128)(2,1)} %constant.2.clone.pick_source), custom_call_target="tpu_custom_call" | custom-call | tf_op jit(solution)/shard_map/pallas_call | solution.py:671
  45.1 1.3 %copy.8 = f32[4,2,320]{2,1,0:T(2,128)} copy(f32[4,2,320]{2,1,0:T(2,128)} %shard_map.64) | data formatting | bytes 20480

commit v2 on v1

--- a/solution.py
+++ b/solution.py
@@ -18,6 +18,7 @@
 SLOTS = (0, EXTENT - 1) + tuple(range(1, EXTENT - 1))
 WIDE = 256
 ROWS = TRACE + 8
+BUDGETS = (1.7, 1.0)
 F32 = jnp.float32
 BF16 = jnp.bfloat16
 
@@ -135,8 +136,8 @@
 
 def kernel(
     layers, cells, width, rounds,
-    inv, vector, lift_maps, jacobians, orient, pick_source, out,
-    blocks, block_sem, lifts, lift_sem, pick, pick_sem, vecs, jac_rows, packed, near,
+    inv, vector_source, lift_maps, jacobian_source, orient, pick_source, out,
+    blocks, block_sem, lifts, lift_sem, pick, pick_sem, vector, jacobians, input_sem, vecs, jac_rows, packed, near,
     ends, sides, inner, full, y, x, entry, climb, reach, zmat, firsts,
     mine, theirs, send_sem, recv_sem, tail_sems, z_mine, z_theirs, z_send, z_recv,
     turns, traces, backs, got_high, got_back, from_left, from_right, cross_sems, natural,
@@ -163,10 +164,27 @@
         ]
 
     early, late = (0, 1), tuple(range(2, EXTENT))
+    def column_of(c):
+        return [at(layer, c) for layer in range(layers)]
+
+    def fetch(members, slots):
+        for e in members:
+            for copy in block_copies(e, slots):
+                copy.start()
+
+    def ready(members, slots):
+        for e in members:
+            for copy in block_copies(e, slots):
+                copy.wait()
+
+    input_copies = [
+        pltpu.make_async_copy(jacobian_source, jacobians, input_sem.at[0]),
+        pltpu.make_async_copy(vector_source, vector, input_sem.at[1]),
+    ]
+    input_copies[1].start()
     lift_copies[0].start()
-    for e in order:
-        for copy in block_copies(e, early):
-            copy.start()
+    fetch(column_of(0), early)
+    input_copies[0].start()
     pick_copy = pltpu.make_async_copy(pick_source, pick, pick_sem.at[0])
 
     bits = [lax.rem(place // (1 << k), 2) for k in range(rounds)]
@@ -185,18 +203,20 @@
 
     vecs[...] = jnp.zeros_like(vecs)
     jac_rows[...] = jnp.zeros_like(jac_rows)
+    backs[...] = jnp.zeros_like(backs)
+
+    def spread_jacobians(c):
+        for e in column_of(c):
+            for v in range(VARS):
+                for w in range(VARS):
+                    jac_rows[e, w, :4, v * FACE : (v + 1) * FACE] = jacobians[e, v, w]
+            for w in range(VARS):
+                value = jac_rows[e, w]
+                jac_rows[e, w] = value + pltpu.roll(value, TRACE, 1) + pltpu.roll(value, 2 * TRACE, 1)
+
+    input_copies[1].wait()
     for e in range(elements):
         vecs[e : e + 1, :] = vector[e // cells, e % cells : e % cells + 1, :]
-        for v in range(VARS):
-            for w in range(VARS):
-                jac_rows[e, w, :4, v * FACE : (v + 1) * FACE] = jacobians[e, v, w]
-        for w in range(VARS):
-            value = jac_rows[e, w]
-            jac_rows[e, w] = value + pltpu.roll(value, TRACE, 1) + pltpu.roll(value, 2 * TRACE, 1)
-    ends[...] = jnp.zeros_like(ends)
-    sides[...] = jnp.zeros_like(sides)
-    y[...] = jnp.zeros_like(y)
-    backs[...] = jnp.zeros_like(backs)
 
     row_face = rows((TRACE, TRACE))
     lane_face = lanes((TRACE, TRACE))
@@ -241,12 +261,12 @@
     lift_copies[0].wait()
     packed[:vec_at] = pack_left(lifts[0:2].reshape(2 * TRACE, BLOCK))
 
-    def critical(e):
+    def passing(e):
         block = half(e, 0)
         near[e] = block
         through = against(packed[:rest_at], block)
         y[0, e : e + 1, :HALF] = through[vec_at + e : vec_at + e + 1]
-        ending(e, 0, through)
+        return through
 
     def rest(e):
         through = against(packed[...], half(e, 1))
@@ -303,6 +323,7 @@
                 both = low(pair)
             else:
                 both = low(multiply(pair[:, :TRACE], behind))
+                yield
             after.append(both[:TRACE])
             behind = both[TRACE:]
         ahead = eye_high
@@ -315,6 +336,7 @@
                     ahead = high(ends[e, 0, TRACE:]) + after[layer]
                 else:
                     ahead = multiply(ends[e, 0, TRACE:, : 2 * TRACE], below(ahead)) + after[layer]
+                    yield
 
     def ordered(k, c):
         flag = bits[k] == 1
@@ -327,14 +349,17 @@
             near, far = eye_low, low(first)
             ahead = eye_high
         else:
-            near, ahead = entry[c, :TRACE], entry[c, TRACE : 2 * TRACE]
+            near, ahead = entry[k, c, :TRACE], entry[k, c, TRACE : 2 * TRACE]
             far = multiply(first[:, :TRACE], near)
         reach[k, c, :TRACE] = jnp.where(flag, 0.0, near)
         reach[k, c, TRACE:] = jnp.where(flag, ahead, far)
 
+    def reach_level(k, c):
+        other = jnp.where(bits[k] == 1, mine[k, c, :TRACE, :128], theirs[k, c, :TRACE, :128])
+        reaching(k, c, jnp.concatenate([other, jnp.zeros((TRACE, WIDE - 128), F32)], axis=1))
+
     def level(k, c):
         left, right = ordered(k, c)
-        reaching(k, c, right[:TRACE])
         flag = bits[k] == 1
         first = firsts[k, c]
         step = jnp.concatenate(
@@ -346,12 +371,15 @@
             axis=0,
         )
         if k == 0:
-            entry[c] = step
+            entry[1, c] = step
         else:
-            old = entry[c]
+            old = entry[k, c]
             moved = multiply(step[:, : 2 * TRACE], old[: 2 * TRACE])
-            entry[c, : 2 * TRACE] = moved[: 2 * TRACE]
-            entry[c, 2 * TRACE :] = moved[2 * TRACE :] + old[2 * TRACE :]
+            entry[k + 1, c, : 2 * TRACE] = moved[: 2 * TRACE]
+            entry[k + 1, c, 2 * TRACE :] = moved[2 * TRACE :] + old[2 * TRACE :]
+
+    def climbing(k, c):
+        left, right = ordered(k, c)
         back = to_low(left[:TRACE])
         climb[k, c, :TRACE] = back
         climb[k, c, TRACE:] = multiply(right[:TRACE, :TRACE], back) + high(right[:TRACE])
@@ -393,29 +421,29 @@
             sent.append(copy)
 
     sides_met = jnp.minimum(column_at, 1) + jnp.minimum(width - 1 - column_at, 1)
-    def column_of(c):
-        return [at(layer, c) for layer in range(layers)]
-
-    def ready(members, slots):
-        for e in members:
-            for copy in block_copies(e, slots):
-                copy.wait()
-
     ready(column_of(0), early)
+    for c in range(1, cells):
+        fetch(column_of(c), early)
     lift_copies[1].start()
-    for e in order:
-        for copy in block_copies(e, late):
-            copy.start()
+    fetch(order, late)
     pick_copy.start()
-    for e in column_of(0):
-        critical(e)
+    throughs = [passing(e) for e in column_of(0)]
+    input_copies[0].wait()
+    spread_jacobians(0)
+    for e, through in zip(column_of(0), throughs):
+        ending(e, 0, through)
     for c in range(cells):
         steps = chain(c)
         if c + 1 < cells:
             ready(column_of(c + 1), early)
+            spread_jacobians(c + 1)
+            throughs = []
             for e in column_of(c + 1):
                 next(steps, None)
-                critical(e)
+                throughs.append(passing(e))
+            for e, through in zip(column_of(c + 1), throughs):
+                next(steps, None)
+                ending(e, 0, through)
         for _ in steps:
             pass
         if c == 0:
@@ -427,29 +455,44 @@
     ready(order, late)
     if rounds == 1:
         for c in range(cells):
-            entry[c] = jnp.concatenate([eye_low, eye_high, jnp.zeros((8, WIDE), F32)], axis=0)
+            entry[0, c] = jnp.concatenate([eye_low, eye_high, jnp.zeros((8, WIDE), F32)], axis=0)
+
+    answering = [responses(c) for c in range(cells)]
+
+    def rest_and_answer(e):
+        for steps in answering:
+            next(steps, None)
+        rest(e)
+
+    def finish_answers():
+        for steps in answering:
+            for _ in steps:
+                pass
 
     tasks = []
+
+    def later(cost, function, *values):
+        tasks.append((cost, functools.partial(function, *values)))
+
     for index, e in enumerate(order):
-        tasks.append(functools.partial(rest, e))
+        later(0.65, rest_and_answer, e)
         if index:
-            tasks.append(functools.partial(finish, order[index - 1]))
-    tasks.append(functools.partial(finish, order[-1]))
+            later(0.2, finish, order[index - 1])
+    later(0.2, finish, order[-1])
+    later(0.05, finish_answers)
     for e in range(elements):
-        tasks.append(functools.partial(turn, e))
-    for c in range(cells):
-        tasks.append(functools.partial(responses, c))
-
-    slots = rounds * cells
-    quota = -(-len(tasks) // slots)
-
-    def work(count):
-        for _ in range(min(count, len(tasks))):
-            tasks.pop(0)()
+        later(0.03, turn, e)
+
+    def work(budget):
+        while tasks and (budget is None or tasks[0][0] <= budget):
+            cost, task = tasks.pop(0)
+            task()
+            if budget is not None:
+                budget -= cost
 
     for k in range(rounds):
         for c in range(cells):
-            work(quota)
+            work(BUDGETS[c > 0])
             for copy in pending[k, c]:
                 copy.wait_recv()
             if k < rounds - 1:
@@ -459,7 +502,7 @@
                 dispatch(k + 1, c)
                 firsts[k, c] = first
                 level(k, c)
-    work(len(tasks))
+    work(None)
 
     top = rounds - 1
     top_flag = bits[top] == 1
@@ -473,8 +516,8 @@
     met, _ = meet(z_ours, z_other, top_flag)
     turned = each(met, [below(low(theirs[top, c, :TRACE])) for c in range(cells)])
     arrived = jnp.where(top_flag, high(met), low(met + turned))
-    z_in = each(arrived, [entry[c, : 2 * TRACE] for c in range(cells)]) + stack(
-        [entry[c, 2 * TRACE : 2 * TRACE + 1] for c in range(cells)]
+    z_in = each(arrived, [entry[top, c, : 2 * TRACE] for c in range(cells)]) + stack(
+        [entry[top, c, 2 * TRACE : 2 * TRACE + 1] for c in range(cells)]
     )
     column = z_in.T
     for layer in range(layers):
@@ -490,7 +533,7 @@
     pick_copy.wait()
     cross = jnp.zeros((elements, WIDE), F32)
     for h in range(2):
-        x_high, x_low = split(x[h])
+        x_high, x_low = split(x[h, :, :HALF])
         cross = cross + (
             jnp.dot(x_high, pick[h], preferred_element_type=F32)
             + jnp.dot(x_low, pick[h], preferred_element_type=F32)
@@ -510,8 +553,9 @@
     def _():
         down.start()
 
-    for c in range(cells):
-        reaching(top, c, jnp.concatenate([theirs[top, c, :TRACE, :128], jnp.zeros((TRACE, WIDE - 128), F32)], axis=1))
+    for k in range(min(2, top)):
+        for c in range(cells):
+            climbing(k, c)
     for layer in range(layers):
         for c in range(cells):
             e = at(layer, c)
@@ -599,17 +643,23 @@
                 for h in range(2):
                     x[h, e : e + 1, :] = y[h, e : e + 1, :] + apply(column[: 2 * TRACE, c : c + 1], ends[e, h])
 
-    tasks = [local_sweeps, local_rest, local_apply]
+    for task in (local_sweeps, local_rest, local_apply):
+        later(0, task)
     z_in = jnp.zeros((8, WIDE), F32)
     for k in range(rounds):
         flag = bits[k] == 1
         copy = remote(z_mine.at[k], z_theirs.at[k], z_send.at[k], z_recv.at[k], (partners[k], column_at))
         copy.start()
         sent.append(copy)
+        for c in range(cells):
+            reach_level(k, c)
+            if 2 <= k + 1 < top:
+                climbing(k + 1, c)
         if k < rounds - 1:
-            work(1)
+            if tasks:
+                tasks.pop(0)[1]()
         else:
-            work(len(tasks))
+            work(None)
         copy.wait_recv()
         met, kept = meet(z_mine[k], z_theirs[k], flag)
         if k < rounds - 1:
@@ -645,7 +695,7 @@
 
 
 def picker():
-    table = np.zeros((2, WIDE, WIDE), np.float32)
+    table = np.zeros((2, HALF, WIDE), np.float32)
     for slot, i in enumerate(SLOTS):
         for v in range(VARS):
             for k in range(EXTENT):
@@ -671,15 +721,18 @@
     result = pl.pallas_call(
         functools.partial(kernel, layers, cells, width, rounds),
         out_shape=jax.ShapeDtypeStruct((layers, cells, BLOCK), F32),
-        in_specs=[hbm, vmem, hbm, vmem, pl.BlockSpec(memory_space=pltpu.SMEM), hbm],
+        in_specs=[hbm, hbm, hbm, hbm, pl.BlockSpec(memory_space=pltpu.SMEM), hbm],
         out_specs=vmem,
         scratch_shapes=[
             pltpu.VMEM((elements, EXTENT, VARS, FACE, BLOCK), F32),
             pltpu.SemaphoreType.DMA((elements, EXTENT)),
             pltpu.VMEM((4, TRACE, BLOCK), F32),
             pltpu.SemaphoreType.DMA((2,)),
-            pltpu.VMEM((2, WIDE, WIDE), BF16),
+            pltpu.VMEM((2, HALF, WIDE), BF16),
             pltpu.SemaphoreType.DMA((1,)),
+            pltpu.VMEM((layers, cells, BLOCK), F32),
+            pltpu.VMEM((elements, VARS, VARS, 4, FACE), F32),
+            pltpu.SemaphoreType.DMA((2,)),
             pltpu.VMEM((vec_rows, BLOCK), F32),
             pltpu.VMEM((elements, VARS, 8, WIDE), F32),
             pltpu.VMEM((depth, 4 * WIDE), BF16),
@@ -690,7 +743,7 @@
             pltpu.VMEM((elements, 2, tall, WIDE), F32),
             pltpu.VMEM((2, elements, WIDE), F32),
             pltpu.VMEM((2, elements, WIDE), F32),
-            pltpu.VMEM((cells, tall, WIDE), F32),
+            pltpu.VMEM((rounds, cells, tall, WIDE), F32),
             pltpu.VMEM((rounds, cells, 2 * TRACE, WIDE), F32),
             pltpu.VMEM((rounds, cells, 2 * TRACE, WIDE), F32),
             pltpu.VMEM((elements, 2 * TRACE, WIDE), F32),

time: 46.7 us -> 43 us (0.921)
  Pallas kernels: 45 us -> 41.5 us
    pallas_call x1, Pallas kernels: 45 us -> 41.5 us  [on_device(): pl.pallas_call(functools.partial(kernel, layers, cells, width, rounds), o...]
where the time goes in v2:
time: 43 us; the launch traced here: 42.8 us
  Pallas kernels  41.5 us (97%)
  local copies, waits for them, and re-layouts  1.31 us (3%)
    pallas_call x1, Pallas kernels, on_device(): pl.pallas_call(functools.partial(kernel, layers, cells, width, rounds), o...  41.5 us
    unnamed x1, local copies, waits for them, and re-layouts  1.31 us

profile of v2, /device:TPU:0, one launch (start us, length us, event | category | flops | bytes accessed | tf_op | source)
XLA Modules:
  0.0 42.8 jit_solution(7501748434763243608)
XLA Ops:
  0.0 41.5 %shard_map.64 = f32[4,2,320]{2,1,0:T(2,128)} custom-call(f32[8,5,4,16,320]{4,3,2,1,0:T(8,128)} %bitcast.6, f32[4,2,320]{2,1,0:T(2,128)} %vector_source.1, f32[4,80,320]{2,1,0:T(8,128)} %bitcast.7, f32[8,5,5,4,16]{4,3,2,1,0:T(4,128)} %bitcast.8, s32[2,4]{1,0:T(2,128)} %bitcast.9, bf16[2,160,256]{2,1,0:T(8,128)(2,1)} %constant.2.clone.pick_source), custom_call_target="tpu_custom_call" | custom-call | tf_op jit(solution)/shard_map/pallas_call | solution.py:721
  41.5 1.3 %copy.8 = f32[4,2,320]{2,1,0:T(2,128)} copy(f32[4,2,320]{2,1,0:T(2,128)} %shard_map.64) | data formatting | bytes 20480

commit v3 on v2

--- a/solution.py
+++ b/solution.py
@@ -18,7 +18,7 @@
 SLOTS = (0, EXTENT - 1) + tuple(range(1, EXTENT - 1))
 WIDE = 256
 ROWS = TRACE + 8
-BUDGETS = (1.7, 1.0)
+BUDGETS = (1.4, 0.7)
 F32 = jnp.float32
 BF16 = jnp.bfloat16
 
@@ -136,9 +136,9 @@
 
 def kernel(
     layers, cells, width, rounds,
-    inv, vector_source, lift_maps, jacobian_source, orient, pick_source, out,
-    blocks, block_sem, lifts, lift_sem, pick, pick_sem, vector, jacobians, input_sem, vecs, jac_rows, packed, near,
-    ends, sides, inner, full, y, x, entry, climb, reach, zmat, firsts,
+    inv, vector_source, lift_maps, jacobian_source, orient_source, pick_source, out,
+    blocks, block_sem, lifts, lift_sem, pick, pick_sem, vector, jacobians, orient, input_sem, vecs, jac_rows, packed, near,
+    ends, sides, inner, full, y, x, entry, climb, climb_got, climb_send, climb_recv, reach, zmat, firsts,
     mine, theirs, send_sem, recv_sem, tail_sems, z_mine, z_theirs, z_send, z_recv,
     turns, traces, backs, got_high, got_back, from_left, from_right, cross_sems, natural,
 ):
@@ -180,18 +180,28 @@
     input_copies = [
         pltpu.make_async_copy(jacobian_source, jacobians, input_sem.at[0]),
         pltpu.make_async_copy(vector_source, vector, input_sem.at[1]),
+        pltpu.make_async_copy(orient_source, orient, input_sem.at[2]),
     ]
     input_copies[1].start()
     lift_copies[0].start()
     fetch(column_of(0), early)
     input_copies[0].start()
+    input_copies[2].start()
     pick_copy = pltpu.make_async_copy(pick_source, pick, pick_sem.at[0])
 
     bits = [lax.rem(place // (1 << k), 2) for k in range(rounds)]
     partners = [place + (1 - 2 * bits[k]) * (1 << k) for k in range(rounds)]
+    paired = min(2, rounds)
+    groups = [tuple(range(paired))] + [(k,) for k in range(paired, rounds)]
+    friends = []
+    for group in groups:
+        near_one, far_one = partners[group[0]], partners[group[-1]]
+        friends.append([near_one, far_one, near_one + far_one - place] if len(group) == 2 else [near_one])
+    met_count = sum(len(friend) for friend in friends)
     barrier = pltpu.get_barrier_semaphore()
-    for k in range(rounds):
-        pl.semaphore_signal(barrier, inc=1, device_id=(partners[k], column_at), device_id_type=pl.DeviceIdType.MESH)
+    for friend in friends:
+        for partner in friend:
+            pl.semaphore_signal(barrier, inc=1, device_id=(partner, column_at), device_id_type=pl.DeviceIdType.MESH)
 
     @pl.when(column_at > 0)
     def _():
@@ -224,6 +234,7 @@
     lane_wide = lax.rem(lanes((TRACE, WIDE)), FACE)
     same = row_wide == lane_wide
     leading = lanes((TRACE, WIDE)) < 2 * TRACE
+    lane_line = lax.rem(lanes((1, WIDE)), FACE)
     eye = rows((TRACE, WIDE)) == lanes((TRACE, WIDE))
     eye_low = eye.astype(F32)
     eye_high = (rows((TRACE, WIDE)) + TRACE == lanes((TRACE, WIDE))).astype(F32)
@@ -268,13 +279,18 @@
         y[0, e : e + 1, :HALF] = through[vec_at + e : vec_at + e + 1]
         return through
 
-    def rest(e):
-        through = against(packed[...], half(e, 1))
+    held = {}
+
+    def rest_pass(e):
+        held[e] = against(packed[...], half(e, 1)), against(packed[rest_at:], near[e])
+
+    def rest_end(e):
+        through, beside = held.pop(e)
         y[1, e : e + 1, :HALF] = through[vec_at + e : vec_at + e + 1]
         ending(e, 1, through)
-        chosen = row_wide == source_of(orient[e % cells, e // cells], lane_wide)
+        chosen = row_wide == source_of(orient[e % cells, e // cells], lane_line)
         faces = face(e, 2, chosen), face(e, 3, same)
-        for h, value in enumerate((against(packed[rest_at:], near[e]), through[rest_at:])):
+        for h, value in enumerate((beside, through[rest_at:])):
             for m in range(2):
                 sides[e, h, m * TRACE : (m + 1) * TRACE, :HALF] = faced(
                     faces[m], value[m * TRACE : (m + 1) * TRACE]
@@ -380,17 +396,20 @@
 
     def climbing(k, c):
         left, right = ordered(k, c)
-        back = to_low(left[:TRACE])
-        climb[k, c, :TRACE] = back
-        climb[k, c, TRACE:] = multiply(right[:TRACE, :TRACE], back) + high(right[:TRACE])
-
-    block_row, block_lane = lax.div(row_face, FACE), lax.div(lane_face, FACE)
-    face_lane = lane_face - block_lane * FACE
+        back = left[:TRACE]
+        turned = low(multiply(right[:TRACE, :TRACE], to_low(back)))
+        climb[k, c] = turned + high(right[:TRACE]) + keep(lanes((TRACE, WIDE)) >= 2 * TRACE, back)
+
+    def climber(packed_climb):
+        return jnp.concatenate([to_low(packed_climb), packed_climb], axis=0)
+
+    alike = lax.div(row_face, FACE) == lax.div(lane_face, FACE)
+    small_row = rows((FACE, TRACE))
+    small_lane = lax.rem(lanes((FACE, TRACE)), FACE)
 
     def turn(e):
-        within = row_face - block_row * FACE
-        chosen = (block_row == block_lane) & (source_of(orient[e % cells, e // cells], within) == face_lane)
-        turns[e] = chosen.astype(F32)
+        chosen = (source_of(orient[e % cells, e // cells], small_row) == small_lane).astype(F32)
+        turns[e] = keep(alike, jnp.concatenate([chosen] * VARS, axis=0))
 
     def remote(source, target, send, recv, device):
         return pltpu.make_async_remote_copy(
@@ -400,6 +419,7 @@
 
     sent = []
     pending = {}
+    climb_copies = {}
 
     def dispatch(k, c):
         device = (partners[k], column_at)
@@ -447,10 +467,11 @@
         for _ in steps:
             pass
         if c == 0:
-            pl.semaphore_wait(barrier, rounds + sides_met)
+            pl.semaphore_wait(barrier, met_count + sides_met)
         dispatch(0, c)
 
     lift_copies[1].wait()
+    input_copies[2].wait()
     packed[rest_at:] = pack_left(lifts[2:4].reshape(2 * TRACE, BLOCK))
     ready(order, late)
     if rounds == 1:
@@ -459,10 +480,15 @@
 
     answering = [responses(c) for c in range(cells)]
 
-    def rest_and_answer(e):
+    def stage(index):
+        if index < elements:
+            rest_pass(order[index])
+        if 0 < index <= elements:
+            rest_end(order[index - 1])
+        if index > 1:
+            finish(order[index - 2])
         for steps in answering:
             next(steps, None)
-        rest(e)
 
     def finish_answers():
         for steps in answering:
@@ -474,11 +500,8 @@
     def later(cost, function, *values):
         tasks.append((cost, functools.partial(function, *values)))
 
-    for index, e in enumerate(order):
-        later(0.65, rest_and_answer, e)
-        if index:
-            later(0.2, finish, order[index - 1])
-    later(0.2, finish, order[-1])
+    for index in range(elements + 2):
+        later(0.65, stage, index)
     later(0.05, finish_answers)
     for e in range(elements):
         later(0.03, turn, e)
@@ -502,6 +525,16 @@
                 dispatch(k + 1, c)
                 firsts[k, c] = first
                 level(k, c)
+                if k == 0 and c == cells - 1:
+                    for other in range(cells):
+                        climbing(k, other)
+                        copy = remote(
+                            climb.at[k, other], climb_got.at[k, other],
+                            climb_send.at[k, other], climb_recv.at[k, other], (partners[k + 1], column_at),
+                        )
+                        copy.start()
+                        sent.append(copy)
+                        climb_copies[k, other] = copy
     work(None)
 
     top = rounds - 1
@@ -553,9 +586,14 @@
     def _():
         down.start()
 
-    for k in range(min(2, top)):
-        for c in range(cells):
-            climbing(k, c)
+    def prepare(g):
+        for k in groups[g]:
+            for c in range(cells):
+                reach_level(k, c)
+                if 0 < k < top:
+                    climbing(k, c)
+
+    prepare(0)
     for layer in range(layers):
         for c in range(cells):
             e = at(layer, c)
@@ -635,7 +673,8 @@
         for e in range(elements):
             y[1, e : e + 1, :] = loaded(e, 1)
 
-    def local_apply():
+    def local_settle():
+        local_rest()
         for layer in range(layers):
             column = state[layer].T
             for c in range(cells):
@@ -643,28 +682,40 @@
                 for h in range(2):
                     x[h, e : e + 1, :] = y[h, e : e + 1, :] + apply(column[: 2 * TRACE, c : c + 1], ends[e, h])
 
-    for task in (local_sweeps, local_rest, local_apply):
+    for task in (local_sweeps, local_settle):
         later(0, task)
     z_in = jnp.zeros((8, WIDE), F32)
-    for k in range(rounds):
-        flag = bits[k] == 1
-        copy = remote(z_mine.at[k], z_theirs.at[k], z_send.at[k], z_recv.at[k], (partners[k], column_at))
-        copy.start()
-        sent.append(copy)
-        for c in range(cells):
-            reach_level(k, c)
-            if 2 <= k + 1 < top:
-                climbing(k + 1, c)
-        if k < rounds - 1:
-            if tasks:
-                tasks.pop(0)[1]()
+    for g, group in enumerate(groups):
+        copies = [
+            remote(z_mine.at[g], z_theirs.at[g, i], z_send.at[g, i], z_recv.at[g, i], (partner, column_at))
+            for i, partner in enumerate(friends[g])
+        ]
+        for copy in copies:
+            copy.start()
+            sent.append(copy)
+        if g + 1 < len(groups):
+            prepare(g + 1)
+            tasks.pop(0)[1]() if tasks else None
         else:
             work(None)
-        copy.wait_recv()
-        met, kept = meet(z_mine[k], z_theirs[k], flag)
-        if k < rounds - 1:
-            z_mine[k + 1] = each(met, [climb[k, c] for c in range(cells)]) + kept
+        k = group[0]
+        if len(group) == 2:
+            for c in range(cells):
+                climb_copies[k, c].wait_recv()
+        for copy in copies:
+            copy.wait_recv()
+        flag = bits[k] == 1
+        met, kept = meet(z_mine[g], z_theirs[g, 0], flag)
         z_in = z_in + each(met, [reach[k, c] for c in range(cells)])
+        if len(group) == 2:
+            both, stays = meet(z_theirs[g, 1], z_theirs[g, 2], flag)
+            ours = kept + each(met, [climber(climb[k, c]) for c in range(cells)])
+            other = stays + each(both, [climber(climb_got[k, c]) for c in range(cells)])
+            k = group[1]
+            met, kept = meet(ours, other, bits[k] == 1)
+            z_in = z_in + each(met, [reach[k, c] for c in range(cells)])
+        if k < top:
+            z_mine[g + 1] = kept + each(met, [climber(climb[k, c]) for c in range(cells)])
 
     column = z_in.T
     for layer in range(layers):
@@ -718,10 +769,11 @@
     vmem = pl.BlockSpec(memory_space=pltpu.VMEM)
     hbm = pl.BlockSpec(memory_space=pltpu.HBM)
     tall = 2 * TRACE + 8
+    groups = max(1, rounds - 1)
     result = pl.pallas_call(
         functools.partial(kernel, layers, cells, width, rounds),
-        out_shape=jax.ShapeDtypeStruct((layers, cells, BLOCK), F32),
-        in_specs=[hbm, hbm, hbm, hbm, pl.BlockSpec(memory_space=pltpu.SMEM), hbm],
+        out_shape=pltpu.VMEM((layers, cells, BLOCK), F32),
+        in_specs=[hbm] * 6,
         out_specs=vmem,
         scratch_shapes=[
             pltpu.VMEM((elements, EXTENT, VARS, FACE, BLOCK), F32),
@@ -732,7 +784,8 @@
             pltpu.SemaphoreType.DMA((1,)),
             pltpu.VMEM((layers, cells, BLOCK), F32),
             pltpu.VMEM((elements, VARS, VARS, 4, FACE), F32),
-            pltpu.SemaphoreType.DMA((2,)),
+            pltpu.SMEM((cells, layers), jnp.int32),
+            pltpu.SemaphoreType.DMA((3,)),
             pltpu.VMEM((vec_rows, BLOCK), F32),
             pltpu.VMEM((elements, VARS, 8, WIDE), F32),
             pltpu.VMEM((depth, 4 * WIDE), BF16),
@@ -744,7 +797,10 @@
             pltpu.VMEM((2, elements, WIDE), F32),
             pltpu.VMEM((2, elements, WIDE), F32),
             pltpu.VMEM((rounds, cells, tall, WIDE), F32),
-            pltpu.VMEM((rounds, cells, 2 * TRACE, WIDE), F32),
+            pltpu.VMEM((rounds, cells, TRACE, WIDE), F32),
+            pltpu.VMEM((rounds, cells, TRACE, WIDE), F32),
+            pltpu.SemaphoreType.DMA((rounds, cells)),
+            pltpu.SemaphoreType.DMA((rounds, cells)),
             pltpu.VMEM((rounds, cells, 2 * TRACE, WIDE), F32),
             pltpu.VMEM((elements, 2 * TRACE, WIDE), F32),
             pltpu.VMEM((rounds, cells, ROWS, WIDE), F32),
@@ -753,10 +809,10 @@
             pltpu.SemaphoreType.DMA((rounds, cells)),
             pltpu.SemaphoreType.DMA((rounds, cells)),
             pltpu.SemaphoreType.DMA((2, cells)),
-            pltpu.VMEM((rounds, 8, WIDE), F32),
-            pltpu.VMEM((rounds, 8, WIDE), F32),
-            pltpu.SemaphoreType.DMA((rounds,)),
-            pltpu.SemaphoreType.DMA((rounds,)),
+            pltpu.VMEM((groups, 8, WIDE), F32),
+            pltpu.VMEM((groups, 3, 8, WIDE), F32),
+            pltpu.SemaphoreType.DMA((groups, 3)),
+            pltpu.SemaphoreType.DMA((groups, 3)),
             pltpu.VMEM((elements, TRACE, TRACE), F32),
             pltpu.VMEM((elements, 128), F32),
             pltpu.VMEM((elements, 128), F32),

time: 43 us -> 39.8 us (0.926)
  Pallas kernels: 41.5 us -> 39.1 us
  local copies, waits for them, and re-layouts: 1.31 us -> 0.6 us
    pallas_call x1, Pallas kernels: 41.5 us -> 39.1 us  [on_device(): pl.pallas_call(functools.partial(kernel, layers, cells, width, rounds), o...]
    unnamed x1, local copies, waits for them, and re-layouts: 1.31 us -> 0.6 us
where the time goes in v3:
time: 39.8 us; the launch traced here: 39.7 us
  Pallas kernels  39.1 us (98%)
  local copies, waits for them, and re-layouts  0.6 us (2%)
    pallas_call x1, Pallas kernels, on_device(): pl.pallas_call(functools.partial(kernel, layers, cells, width, rounds), o...  39.1 us

profile of v3, /device:TPU:0, one launch (start us, length us, event | category | flops | bytes accessed | tf_op | source)
XLA Modules:
  0.0 39.7 jit_solution(12643214663410047201)
XLA Ops:
  0.0 39.1 %shard_map.64 = f32[4,2,320]{2,1,0:T(2,128)S(1)} custom-call(f32[8,5,4,16,320]{4,3,2,1,0:T(8,128)} %bitcast.6, f32[4,2,320]{2,1,0:T(2,128)} %vector_source.1, f32[4,80,320]{2,1,0:T(8,128)} %bitcast.7, f32[8,5,5,4,16]{4,3,2,1,0:T(4,128)} %bitcast.8, s32[2,4]{1,0:T(2,128)} %bitcast.9, bf16[2,160,256]{2,1,0:T(8,128)(2,1)} %constant.2.clone.pick_source), custom_call_target="tpu_custom_call" | custom-call | tf_op jit(solution)/shard_map/pallas_call | solution.py:773
  39.1 0.6 %copy.8 = f32[4,2,320]{2,1,0:T(2,128)} copy(f32[4,2,320]{2,1,0:T(2,128)S(1)} %shard_map.64) | data formatting | bytes 20480

commit v4 on v3

--- a/solution.py
+++ b/solution.py
@@ -18,7 +18,6 @@
 SLOTS = (0, EXTENT - 1) + tuple(range(1, EXTENT - 1))
 WIDE = 256
 ROWS = TRACE + 8
-BUDGETS = (1.4, 0.7)
 F32 = jnp.float32
 BF16 = jnp.bfloat16
 
@@ -138,7 +137,7 @@
     layers, cells, width, rounds,
     inv, vector_source, lift_maps, jacobian_source, orient_source, pick_source, out,
     blocks, block_sem, lifts, lift_sem, pick, pick_sem, vector, jacobians, orient, input_sem, vecs, jac_rows, packed, near,
-    ends, sides, inner, full, y, x, entry, climb, climb_got, climb_send, climb_recv, reach, zmat, firsts,
+    ends, sides, inner, full, y, x, entry, climb, climb_got, climb_send, climb_recv, reach, zmat, drop, firsts,
     mine, theirs, send_sem, recv_sem, tail_sems, z_mine, z_theirs, z_send, z_recv,
     turns, traces, backs, got_high, got_back, from_left, from_right, cross_sems, natural,
 ):
@@ -182,10 +181,10 @@
         pltpu.make_async_copy(vector_source, vector, input_sem.at[1]),
         pltpu.make_async_copy(orient_source, orient, input_sem.at[2]),
     ]
+    lift_copies[0].start()
     input_copies[1].start()
-    lift_copies[0].start()
+    input_copies[0].start()
     fetch(column_of(0), early)
-    input_copies[0].start()
     input_copies[2].start()
     pick_copy = pltpu.make_async_copy(pick_source, pick, pick_sem.at[0])
 
@@ -224,9 +223,6 @@
                 value = jac_rows[e, w]
                 jac_rows[e, w] = value + pltpu.roll(value, TRACE, 1) + pltpu.roll(value, 2 * TRACE, 1)
 
-    input_copies[1].wait()
-    for e in range(elements):
-        vecs[e : e + 1, :] = vector[e // cells, e % cells : e % cells + 1, :]
 
     row_face = rows((TRACE, TRACE))
     lane_face = lanes((TRACE, TRACE))
@@ -268,9 +264,13 @@
         ends[e, h, :TRACE, :HALF] = -faced(face(e, 1, same), through[TRACE : 2 * TRACE])
 
     vec_at, rest_at = 2 * TRACE, 2 * TRACE + vec_rows
-    packed[vec_at:rest_at] = pack_left(vecs[...])
     lift_copies[0].wait()
     packed[:vec_at] = pack_left(lifts[0:2].reshape(2 * TRACE, BLOCK))
+    input_copies[1].wait()
+    for e in range(elements):
+        vecs[e : e + 1, :] = vector[e // cells, e % cells : e % cells + 1, :]
+    packed[vec_at:rest_at] = pack_left(vecs[...])
+    input_copies[0].wait()
 
     def passing(e):
         block = half(e, 0)
@@ -448,7 +448,6 @@
     fetch(order, late)
     pick_copy.start()
     throughs = [passing(e) for e in column_of(0)]
-    input_copies[0].wait()
     spread_jacobians(0)
     for e, through in zip(column_of(0), throughs):
         ending(e, 0, through)
@@ -495,6 +494,9 @@
             for _ in steps:
                 pass
 
+    def compose(e):
+        drop[e] = multiply(sides[e, 0, :, :HALF], zmat[e])
+
     tasks = []
 
     def later(cost, function, *values):
@@ -505,6 +507,8 @@
     later(0.05, finish_answers)
     for e in range(elements):
         later(0.03, turn, e)
+    for e in range(elements):
+        later(0.1, compose, e)
 
     def work(budget):
         while tasks and (budget is None or tasks[0][0] <= budget):
@@ -515,7 +519,7 @@
 
     for k in range(rounds):
         for c in range(cells):
-            work(BUDGETS[c > 0])
+            work(None if k == rounds - 1 and c == cells - 1 else 2.0 if k == c == 0 else 0.7)
             for copy in pending[k, c]:
                 copy.wait_recv()
             if k < rounds - 1:
@@ -635,14 +639,13 @@
             + apply(right_columns[:TRACE, e : e + 1], sides[e, h, TRACE:])
         )
 
-    for e in range(elements):
-        y[0, e : e + 1, :] = loaded(e, 0)
-    columns = y[0].T
+    def dropped(e):
+        return apply(left_columns[:TRACE, e : e + 1], drop[e, :TRACE]) + apply(
+            right_columns[:TRACE, e : e + 1], drop[e, TRACE:]
+        )
+
     z_mine[0] = stack([
-        functools.reduce(
-            jnp.add,
-            [apply(columns[: 2 * TRACE, at(layer, c) : at(layer, c) + 1], zmat[at(layer, c)]) for layer in range(layers)],
-        )
+        mine[0, c, TRACE : TRACE + 1] - functools.reduce(jnp.add, [dropped(at(layer, c)) for layer in range(layers)])
         for c in range(cells)
     ])
 
@@ -652,6 +655,8 @@
         return stack([y[0, at(layer, c) : at(layer, c) + 1, :] for c in range(cells)])
 
     def local_sweeps():
+        for e in range(elements):
+            y[0, e : e + 1, :] = loaded(e, 0)
         forward = [gathered(0)]
         for layer in range(1, layers):
             step = each(forward[-1], [below(ends[at(layer, c), 0, TRACE:]) for c in range(cells)])
@@ -803,6 +808,7 @@
             pltpu.SemaphoreType.DMA((rounds, cells)),
             pltpu.VMEM((rounds, cells, 2 * TRACE, WIDE), F32),
             pltpu.VMEM((elements, 2 * TRACE, WIDE), F32),
+            pltpu.VMEM((elements, 2 * TRACE, WIDE), F32),
             pltpu.VMEM((rounds, cells, ROWS, WIDE), F32),
             pltpu.VMEM((rounds, cells, ROWS, WIDE), F32),
             pltpu.VMEM((rounds, cells, ROWS, WIDE), F32),

time: 39.8 us -> 39.2 us (0.985)
  Pallas kernels: 39.1 us -> 38.5 us
    pallas_call x1, Pallas kernels: 39.1 us -> 38.5 us  [on_device(): pl.pallas_call(functools.partial(kernel, layers, cells, width, rounds), o...]
where the time goes in v4:
time: 39.2 us; the launch traced here: 39.1 us
  Pallas kernels  38.5 us (98%)
  local copies, waits for them, and re-layouts  0.6 us (2%)
    pallas_call x1, Pallas kernels, on_device(): pl.pallas_call(functools.partial(kernel, layers, cells, width, rounds), o...  38.5 us

profile of v4, /device:TPU:0, one launch (start us, length us, event | category | flops | bytes accessed | tf_op | source)
XLA Modules:
  0.0 39.1 jit_solution(14190273928623133357)
XLA Ops:
  0.0 38.5 %shard_map.64 = f32[4,2,320]{2,1,0:T(2,128)S(1)} custom-call(f32[8,5,4,16,320]{4,3,2,1,0:T(8,128)} %bitcast.6, f32[4,2,320]{2,1,0:T(2,128)} %vector_source.1, f32[4,80,320]{2,1,0:T(8,128)} %bitcast.7, f32[8,5,5,4,16]{4,3,2,1,0:T(4,128)} %bitcast.8, s32[2,4]{1,0:T(2,128)} %bitcast.9, bf16[2,160,256]{2,1,0:T(8,128)(2,1)} %constant.2.clone.pick_source), custom_call_target="tpu_custom_call" | custom-call | tf_op jit(solution)/shard_map/pallas_call | solution.py:778
  38.5 0.6 %copy.8 = f32[4,2,320]{2,1,0:T(2,128)} copy(f32[4,2,320]{2,1,0:T(2,128)S(1)} %shard_map.64) | data formatting | bytes 20480

commit v5 on v4

--- a/solution.py
+++ b/solution.py
@@ -103,13 +103,16 @@
     lane_all = lanes((ROWS, WIDE))
     row_all = rows((ROWS, WIDE))
     first = first + keep((lane_all >= 2 * TRACE) | (row_all >= TRACE), right)
-    back = left[:TRACE]
     through = jnp.concatenate(
-        [to_low(back), jnp.zeros((TRACE, WIDE), F32), keep(lane >= 2 * TRACE, back)], axis=0
+        [jnp.zeros((2 * TRACE, WIDE), F32), keep(lane >= 2 * TRACE, left[:TRACE])], axis=0
     )
-    second = multiply(first[:, : 3 * TRACE], through)
-    middle = (lane_all >= TRACE) & (lane_all < 2 * TRACE)
-    return first, second + keep(middle, first) + keep(lane_all < TRACE, left)
+    passed = multiply(right[:TRACE, : 3 * TRACE], through)
+    upper = high(first) + jnp.concatenate([passed, jnp.zeros((8, WIDE), F32)], axis=0)
+    return first, upper
+
+
+def join_low(left, first):
+    return multiply(first[:, :TRACE], to_low(left[:TRACE])) + low(left)
 
 
 def apply(column, matrix):
@@ -138,7 +141,7 @@
     inv, vector_source, lift_maps, jacobian_source, orient_source, pick_source, out,
     blocks, block_sem, lifts, lift_sem, pick, pick_sem, vector, jacobians, orient, input_sem, vecs, jac_rows, packed, near,
     ends, sides, inner, full, y, x, entry, climb, climb_got, climb_send, climb_recv, reach, zmat, drop, firsts,
-    mine, theirs, send_sem, recv_sem, tail_sems, z_mine, z_theirs, z_send, z_recv,
+    mine, theirs, send_sem, recv_sem, z_mine, z_theirs, z_send, z_recv,
     turns, traces, backs, got_high, got_back, from_left, from_right, cross_sems, natural,
 ):
     elements = layers * cells
@@ -421,24 +424,21 @@
     pending = {}
     climb_copies = {}
 
-    def dispatch(k, c):
+    def dispatch(k, c, part):
         device = (partners[k], column_at)
-        send, recv = send_sem.at[k, c], recv_sem.at[k, c]
-        if k < rounds - 1:
-            pending[k, c] = [remote(mine.at[k, c], theirs.at[k, c], send, recv, device)]
+        if part == 0:
+            held_rows, held_lanes = pl.ds(0, ROWS), pl.ds(0, 128)
+        elif k < rounds - 1:
+            held_rows, held_lanes = pl.ds(0, ROWS), pl.ds(128, 128)
         else:
-            one, two = pl.ds(0, 128), pl.ds(128, 128)
-            foot = pl.ds(TRACE, 8)
-            pending[k, c] = [
-                remote(mine.at[k, c, :, one], theirs.at[k, c, :, one], send, recv, device),
-                remote(
-                    mine.at[k, c, foot, two], theirs.at[k, c, foot, two],
-                    tail_sems.at[0, c], tail_sems.at[1, c], device,
-                ),
-            ]
-        for copy in pending[k, c]:
-            copy.start()
-            sent.append(copy)
+            held_rows, held_lanes = pl.ds(TRACE, 8), pl.ds(128, 128)
+        copy = remote(
+            mine.at[k, c, held_rows, held_lanes], theirs.at[k, c, held_rows, held_lanes],
+            send_sem.at[k, c, part], recv_sem.at[k, c, part], device,
+        )
+        copy.start()
+        sent.append(copy)
+        pending.setdefault((k, c), []).append(copy)
 
     sides_met = jnp.minimum(column_at, 1) + jnp.minimum(width - 1 - column_at, 1)
     ready(column_of(0), early)
@@ -467,7 +467,8 @@
             pass
         if c == 0:
             pl.semaphore_wait(barrier, met_count + sides_met)
-        dispatch(0, c)
+        dispatch(0, c, 1)
+        dispatch(0, c, 0)
 
     lift_copies[1].wait()
     input_copies[2].wait()
@@ -524,9 +525,11 @@
                 copy.wait_recv()
             if k < rounds - 1:
                 left, right = ordered(k, c)
-                first, node = join(left, right)
-                mine[k + 1, c] = node
-                dispatch(k + 1, c)
+                first, upper = join(left, right)
+                mine[k + 1, c, :, 128:] = upper[:, 128:]
+                dispatch(k + 1, c, 1)
+                mine[k + 1, c, :, :128] = (upper + join_low(left, first))[:, :128]
+                dispatch(k + 1, c, 0)
                 firsts[k, c] = first
                 level(k, c)
                 if k == 0 and c == cells - 1:
@@ -812,9 +815,8 @@
             pltpu.VMEM((rounds, cells, ROWS, WIDE), F32),
             pltpu.VMEM((rounds, cells, ROWS, WIDE), F32),
             pltpu.VMEM((rounds, cells, ROWS, WIDE), F32),
-            pltpu.SemaphoreType.DMA((rounds, cells)),
-            pltpu.SemaphoreType.DMA((rounds, cells)),
-            pltpu.SemaphoreType.DMA((2, cells)),
+            pltpu.SemaphoreType.DMA((rounds, cells, 2)),
+            pltpu.SemaphoreType.DMA((rounds, cells, 2)),
             pltpu.VMEM((groups, 8, WIDE), F32),
             pltpu.VMEM((groups, 3, 8, WIDE), F32),
             pltpu.SemaphoreType.DMA((groups, 3)),

time: 39.2 us -> 39.1 us (level)
  no operation moved by 1% of the time
where the time goes in v5:
time: 39.1 us; the launch traced here: 38.9 us
  Pallas kernels  38.3 us (98%)
  local copies, waits for them, and re-layouts  0.6 us (2%)
    pallas_call x1, Pallas kernels, on_device(): pl.pallas_call(functools.partial(kernel, layers, cells, width, rounds), o...  38.3 us

profile of v5, /device:TPU:0, one launch (start us, length us, event | category | flops | bytes accessed | tf_op | source)
XLA Modules:
  0.0 38.9 jit_solution(2979150143994849478)
XLA Ops:
  0.0 38.3 %shard_map.64 = f32[4,2,320]{2,1,0:T(2,128)S(1)} custom-call(f32[8,5,4,16,320]{4,3,2,1,0:T(8,128)} %bitcast.6, f32[4,2,320]{2,1,0:T(2,128)} %vector_source.1, f32[4,80,320]{2,1,0:T(8,128)} %bitcast.7, f32[8,5,5,4,16]{4,3,2,1,0:T(4,128)} %bitcast.8, s32[2,4]{1,0:T(2,128)} %bitcast.9, bf16[2,160,256]{2,1,0:T(8,128)(2,1)} %constant.2.clone.pick_source), custom_call_target="tpu_custom_call" | custom-call | tf_op jit(solution)/shard_map/pallas_call | solution.py:781
  38.3 0.6 %copy.8 = f32[4,2,320]{2,1,0:T(2,128)} copy(f32[4,2,320]{2,1,0:T(2,128)S(1)} %shard_map.64) | data formatting | bytes 20480
